TPU v7x, 512 devices: a whole 4x8x8 slice. The times are simulated.
512 devices in a mesh: row: 32 (over y, x), col: 16 (over z, core).
Axes of the slice: x: 4, y: 8, z: 8, core: 2. Of those that a mesh axis runs over, the one named last changes fastest.
Arguments:
- prior_sample_fields: float32 [128, 256, 4096], P(None, 'row', 'col'), may hold values from -6 to 6
- spreading_coefficient: float32 [256, 4096], P('row', 'col'), may hold values from 0.02 to 0.12
- transport_courant: float32 [2, 256, 4096], P(None, 'row', 'col'), may hold values from 0 to 0.18
- obs_cells: int32 [65536], P(('row', 'col')), may hold values from 0 to 2047
- obs_value: float32 [65536], P(('row', 'col')), may hold values from -6 to 6
- obs_error: float32 [65536], P(('row', 'col')), may hold values from 4 to 32
Outputs:
- analysis: float32 [128, 256, 4096], P(None, 'row', 'col')
All inputs are finite; a program needn't handle non-finite values.
Results may differ from a plain program's by a relative error of at most 0.00011.
Values sent between devices are 32-bit elements; how exact they have to be, the bound alone decides.
A program may use at most 64 MiB of HBM per device.

v0:
```python
import jax
import jax.numpy as jnp
from jax import lax
from jax.sharding import Mesh
from jax.sharding import PartitionSpec as P

ROW_COL = ("row_0", "row_1", "col_0", "col_1")
ROW = ("row_0", "row_1")
COL = ("col_0", "col_1")


def with_halo(x, sides, width):
    for axis, dim in sides:
        devices, length = (lax.axis_size(axis), x.shape[dim])
        up = [(i, (i + 1) % devices) for i in range(devices - 1)]
        down = [(j, i) for i, j in up]
        last = lax.slice_in_dim(x, length - width, length, axis=dim)
        first = lax.slice_in_dim(x, 0, width, axis=dim)
        before = lax.ppermute(last, axis, up)
        after = lax.ppermute(first, axis, down)
        x = jnp.concatenate([before, x, after], axis=dim)
    return x


def cut_along(x, dim, devices):
    before, after = (x.shape[:dim], x.shape[dim + 1 :])
    return jnp.moveaxis(x.reshape(*before, devices, -1, *after), dim, 0)


def sent_and_summed(x, axis, dim):
    devices = lax.axis_size(axis)
    parts = lax.all_to_all(cut_along(x, dim, devices), axis, 0, 0, tiled=True)
    return jnp.sum(parts, axis=0)


def summed_rows(x, axes, dim):
    far, near = axes
    parts = cut_along(x, dim, lax.axis_size(far))
    nearer = sent_and_summed(parts, near, dim + 1)
    arrived = lax.all_to_all(nearer, far, split_axis=0, concat_axis=0, tiled=True)
    return arrived.sum(axis=0)


def rows_for(lines, devices):
    spare = -len(lines) % devices
    return jnp.pad(lines, [(0, spare)] + [(0, 0)] * (lines.ndim - 1))


def from_everyone(x, axis):
    copies = jnp.broadcast_to(x, (lax.axis_size(axis), *x.shape))
    return lax.all_to_all(copies, axis, split_axis=0, concat_axis=0, tiled=True)


def laid_out(parts, dim):
    lengths = list(parts.shape[1:])
    lengths[dim] *= parts.shape[0]
    return jnp.moveaxis(parts, 0, dim).reshape(lengths)


def gather_axes(x, axes, dim):
    far, near = axes
    first = from_everyone(x, far)
    parts = jnp.swapaxes(from_everyone(first, near), 0, 1)
    return laid_out(parts.reshape(-1, *x.shape), dim)


def sum_by_parts(x, axes):
    own = summed_rows(rows_for(x, lax.axis_size(axes[0]) * lax.axis_size(axes[1])), axes, 0)
    whole = gather_axes(own, axes, 0)
    return whole[: len(x)].reshape(x.shape)


def together(arrays, axis):
    ends = [0]
    for a in arrays:
        ends.append(ends[-1] + a.size)
    running = sum_by_parts(jnp.concatenate([a.ravel() for a in arrays]), axis)
    return tuple((running[b:e].reshape(a.shape) for a, b, e in zip(arrays, ends, ends[1:])))


def propagate_dynamics(padded, spreading_coefficient, transport_courant):
    centre = padded[:, 1:-1, 1:-1]
    upper = padded[:, :-2, 1:-1]
    lower = padded[:, 2:, 1:-1]
    left_side = padded[:, 1:-1, :-2]
    right_side = padded[:, 1:-1, 2:]
    spread = upper + lower + left_side + right_side - 4.0 * centre
    return (
        centre
        + spreading_coefficient * spread
        - transport_courant[0] * (centre - upper)
        - transport_courant[1] * (centre - left_side)
    )


def upper_factor(product):
    extent = product.shape[0]
    places = jnp.arange(extent, dtype=jnp.int32)

    def column_step(index, lower_rows):
        row_now = lax.dynamic_slice_in_dim(lower_rows, index, 1, 0)[0]
        column = lax.dynamic_slice_in_dim(product, index, 1, 1)[:, 0] - jnp.dot(
            lower_rows, row_now, precision=lax.Precision.HIGHEST
        )
        pivot = jnp.sqrt(lax.dynamic_slice_in_dim(column, index, 1, 0)[0])
        fresh = jnp.where(places >= index, column / pivot, jnp.float32(0.0))
        return lax.dynamic_update_slice_in_dim(lower_rows, fresh[:, None], index, 1)

    lower_rows = lax.fori_loop(0, extent, column_step, jnp.zeros((extent, extent), jnp.float32))
    return lower_rows.T


def upper_inverse(factor):
    extent = factor.shape[0]
    places = jnp.arange(extent, dtype=jnp.int32)

    def row_step(count, inverse):
        index = extent - 1 - count
        row_now = lax.dynamic_slice_in_dim(factor, index, 1, 0)[0]
        pivot = lax.dynamic_slice_in_dim(row_now, index, 1, 0)[0]
        masked = jnp.where(places > index, row_now, jnp.float32(0.0))
        unit_row = (places == index).astype(jnp.float32)
        fresh = (unit_row - jnp.dot(masked, inverse, precision=lax.Precision.HIGHEST)) / pivot
        return lax.dynamic_update_slice_in_dim(inverse, fresh[None, :], index, 0)

    return lax.fori_loop(0, extent, row_step, jnp.zeros((extent, extent), jnp.float32))


def body(
    prior_sample_fields, spreading_coefficient, transport_courant, obs_cells, obs_value, obs_error
):
    sample_total = prior_sample_fields.shape[0]
    stacked = jnp.concatenate(
        [prior_sample_fields, spreading_coefficient[None], transport_courant], axis=0
    )
    widened = with_halo(stacked, ((ROW, 1), (COL, 2)), 2)
    members = widened[:sample_total]
    coeffs = widened[sample_total:, 1:-1, 1:-1]
    inner_field_block = propagate_dynamics(members, coeffs[0], coeffs[1:])
    predicted_fields = propagate_dynamics(
        inner_field_block, spreading_coefficient, transport_courant
    )
    raveled_field_vector = predicted_fields.reshape(sample_total, -1)
    cell_total = raveled_field_vector.shape[1]
    selector = (jnp.arange(cell_total, dtype=jnp.int32)[:, None] == obs_cells[None, :]).astype(
        jnp.float32
    )
    measurement_vector = jnp.dot(raveled_field_vector, selector, precision=lax.Precision.HIGHEST)
    sample_centroid = jnp.mean(predicted_fields, axis=0)
    sample_departures = raveled_field_vector - sample_centroid.reshape(1, -1)
    obs_mean = jnp.mean(measurement_vector, axis=0)
    root = jnp.sqrt(jnp.float32(sample_total - 1))
    scaled = (measurement_vector - obs_mean) / (obs_error * root)
    innovation = (obs_value - obs_mean) / obs_error
    eye = jnp.eye(sample_total, dtype=jnp.float32)
    pull_part = jnp.dot(scaled, innovation[:, None], precision=lax.Precision.HIGHEST)
    gram_part = jnp.dot(scaled, scaled.T, precision=lax.Precision.HIGHEST)
    gram_total, pulled = together((gram_part, pull_part), ("row_0", ("row_1", "col_0", "col_1")))
    factor = upper_factor(eye + gram_total)
    inverse = upper_inverse(factor)
    middle = jnp.dot(inverse.T, pulled, precision=lax.Precision.HIGHEST)
    shift = jnp.dot(inverse, middle, precision=lax.Precision.HIGHEST)
    weights = (shift + inverse) / root
    assimilate_measurements = jnp.dot(weights.T, sample_departures, precision=lax.Precision.HIGHEST)
    return sample_centroid + assimilate_measurements.reshape(predicted_fields.shape)


def solution(mesh):
    split = Mesh(mesh.devices.reshape(8, 4, 8, 2), ("row_0", "row_1", "col_0", "col_1"))
    return jax.shard_map(
        body,
        mesh=split,
        in_specs=(
            P(None, ROW, COL),
            P(ROW, COL),
            P(None, ROW, COL),
            P(ROW_COL),
            P(ROW_COL),
            P(ROW_COL),
        ),
        out_specs=P(None, ROW, COL),
        check_vma=False,
    )
```

profile of v0, /device:TPU:1, one launch (start us, length us, event | category | flops | bytes accessed | tf_op | source)
XLA Modules:
  0.0 564.8 jit_solution(14313734312501492247)
XLA Ops:
  0.0 1.9 pad_maximum_fusion.14
  1.9 4.0 collective-permute-start
  5.9 1.3 collective-permute-start.1
  7.2 2.1 collective-permute-done
  9.5 3.7 collective-permute-done.1
  14.9 7.6 %collective-permute-start.2 = (f32[131,12,2]{0,1,2:T(8,128)S(1)}, f32[131,12,2]{0,1,2:T(8,128)S(1)}, u32[]{:S(2)}, u32[]{:S(2)}) collective-permute-start(f32[131,12,2]{0,1,2:T(8,128)S(1)} %copy.39), channel_id=1, source_target_pairs={{0,1},{1,2},{2,3},{3,4},{4,5},{5,6},{6,7},{7,8},{8,9},{9,10},{10,1... | collective-permute-start | bytes 37736 | tf_op jit(solution)/shard_map/ppermute | solution.py:19
  23.1 2.1 collective-permute-start.3
  26.0 2.4 collective-permute-done.3
  28.5 1.5 copy.42
  31.1 4.4 pad_maximum_fusion
  35.5 7.9 %fusion.25 = f32[128,10,258]{2,1,0:T(8,128)S(1)} fusion(f32[131,12,2]{2,1,0:T(8,128)S(1)} %copy.42, f32[131,2,256]{2,1,0:T(2,128)S(1)} %copy-done.2, f32[131,2,256]{2,1,0:T(2,128)S(1)} %copy.37, f32[2,8,256]{2,1,0:T(8,128)S(1)} %copy-done.3, f32[1,8,256]{2,1,0:T(8,128)S(1)} %bitcast.114, f32[128,8,256]{2,1,0:T(8,128)S(1)} %copy-done, ...), kind=kLoop, calls=%fused_computation.29 | loop fusion | flops 7595520 | bytes 6949680 | tf_op jit(solution)/shard_map/sub | solution.py:89
  43.4 1.2 fusion.43
  47.9 14.6 %all-to-all-start = ((f32[64,1,264]{2,1,0:T(1,128)}), f32[64,1,264]{2,1,0:T(1,128)S(1)}, u32[]{:S(2)}, u32[]{:S(2)}) async-start(f32[64,1,264]{2,1,0:T(1,128)} %reshape.63), calls=%async_computation | async-start | bytes 196608 | tf_op jit(solution)/shard_map/all_to_all | solution.py:32
  62.6 10.2 %all-to-all-done = f32[64,1,264]{2,1,0:T(1,128)S(1)} async-done(((f32[64,1,264]{2,1,0:T(1,128)}), f32[64,1,264]{2,1,0:T(1,128)S(1)}, u32[]{:S(2)}, u32[]{:S(2)}) %all-to-all-start) | async-done | bytes 67616 | tf_op jit(solution)/shard_map/all_to_all | solution.py:32
  74.9 7.0 %all-to-all-start.1 = ((f32[8,1,33]{2,1,0:T(1,128)}), f32[8,1,33]{2,1,0:T(1,128)S(1)}, u32[]{:S(2)}, u32[]{:S(2)}) async-start(f32[8,1,33]{2,1,0:T(1,128)} %bitcast.11), calls=%async_computation.1 | async-start | bytes 8192 | tf_op jit(solution)/shard_map/all_to_all | solution.py:40
  82.0 6.5 %all-to-all-done.1 = f32[8,1,33]{2,1,0:T(1,128)S(1)} async-done(((f32[8,1,33]{2,1,0:T(1,128)}), f32[8,1,33]{2,1,0:T(1,128)S(1)}, u32[]{:S(2)}, u32[]{:S(2)}) %all-to-all-start.1) | async-done | bytes 1088 | tf_op jit(solution)/shard_map/all_to_all | solution.py:40
  89.1 3.3 all-to-all-start.2
  92.4 6.4 %all-to-all-done.2 = f32[8,1,33]{2,1,0:T(1,128)S(1)} async-done(((f32[8,1,33]{2,1,0:T(1,128)}), f32[8,1,33]{2,1,0:T(1,128)S(1)}, u32[]{:S(2)}, u32[]{:S(2)}) %all-to-all-start.2) | async-done | bytes 1088 | tf_op jit(solution)/shard_map/all_to_all | solution.py:51
  99.7 7.2 %all-to-all-start.3 = ((f32[64,1,264]{2,1,0:T(1,128)}), f32[64,1,264]{2,1,0:T(1,128)S(1)}, u32[]{:S(2)}, u32[]{:S(2)}) async-start(f32[64,1,264]{2,1,0:T(1,128)} %reshape.65), calls=%async_computation.3 | async-start | bytes 196608 | tf_op jit(solution)/shard_map/all_to_all | solution.py:51
  107.3 9.9 %all-to-all-done.3 = f32[64,1,264]{2,1,0:T(1,128)S(1)} async-done(((f32[64,1,264]{2,1,0:T(1,128)}), f32[64,1,264]{2,1,0:T(1,128)S(1)}, u32[]{:S(2)}, u32[]{:S(2)}) %all-to-all-start.3) | async-done | bytes 67616 | tf_op jit(solution)/shard_map/all_to_all | solution.py:51
  118.9 257.4 %while.32 = (s32[]{:T(128)}, f32[128,128]{1,0:T(8,128)S(1)}, f32[128,128]{0,1:T(8,128)S(1)}, s32[]{:T(128)}, s32[]{:T(128)}) while((s32[]{:T(128)}, f32[128,128]{1,0:T(8,128)S(1)}, f32[128,128]{0,1:T(8,128)S(1)}, s32[]{:T(128)}, s32[]{:T(128)}) %tuple.82), condition=%wide.region_5.6_spmd.clone, body=%wide.region_4.5_spmd.clone.sunk | while | flops 197122 | bytes 71261 | solution.py:109
  376.4 185.3 %while.33 = (s32[]{:T(128)}, f32[128,128]{1,0:T(8,128)S(1)}, f32[128,128]{1,0:T(8,128)S(1)}, s32[]{:T(128)}, s32[]{:T(128)}, /*index=5*/s32[]{:T(128)}, s32[]{:T(128)}) while((s32[]{:T(128)}, f32[128,128]{1,0:T(8,128)S(1)}, f32[128,128]{1,0:T(8,128)S(1)}, s32[]{:T(128)}, s32[]{:T(128)}, /*index=5*/s32[]{:T(128)}, ...), condition=%wide.region_7.8_spmd.clone.clone, body=%wide.region_6.7_spmd.clone.clone.sunk | while | flops 197383 | bytes 69279 | solution.py:126
  562.0 1.2 convolution_add_fusion
  563.2 1.6 copy.52
  (1085 shorter events, 359.7 us)
Async XLA Ops:
  0.0 13.4 %copy-start.4 = (f32[8,256]{1,0:T(8,128)S(1)}, f32[8,256]{1,0:T(8,128)}, u32[]{:S(2)}) copy-start(f32[8,256]{1,0:T(8,128)} %param.11) | copy-start | bytes 24580
  0.0 13.4 %copy-start = (f32[128,8,256]{2,1,0:T(8,128)S(1)}, f32[128,8,256]{2,1,0:T(8,128)}, u32[]{:S(2)}) copy-start(f32[128,8,256]{2,1,0:T(8,128)} %param.10) | copy-start | bytes 3145732
  0.0 13.4 %copy-start.3 = (f32[2,8,256]{2,1,0:T(8,128)S(1)}, f32[2,8,256]{2,1,0:T(8,128)}, u32[]{:S(2)}) copy-start(f32[2,8,256]{2,1,0:T(8,128)} %param.12) | copy-start | bytes 49156
  1.9 7.4 %collective-permute-start = (f32[131,2,256]{2,0,1:T(8,128)S(1)}, f32[131,2,256]{2,0,1:T(8,128)S(1)}, u32[]{:S(2)}, u32[]{:S(2)}) collective-permute-start(f32[131,2,256]{2,0,1:T(8,128)S(1)} %copy.35), channel_id=1, source_target_pairs={{0,16},{16,32},{32,48},{48,64},{64,80},{80,96},{96,112},{112,128},... | collective-permute-start | bytes 804872 | tf_op jit(solution)/shard_map/ppermute | solution.py:19
  5.9 7.3 %collective-permute-start.1 = (f32[131,2,256]{2,0,1:T(8,128)S(1)}, f32[131,2,256]{2,0,1:T(8,128)S(1)}, u32[]{:S(2)}, u32[]{:S(2)}) collective-permute-start(f32[131,2,256]{2,0,1:T(8,128)S(1)} %copy.36), channel_id=1, source_target_pairs={{16,0},{32,16},{48,32},{64,48},{80,64},{96,80},{112,96},{128,112},... | collective-permute-start | bytes 804872 | tf_op jit(solution)/shard_map/ppermute | solution.py:20
  13.4 0.8 copy-start.1
  14.9 10.4 %collective-permute-start.2 = (f32[131,12,2]{0,1,2:T(8,128)S(1)}, f32[131,12,2]{0,1,2:T(8,128)S(1)}, u32[]{:S(2)}, u32[]{:S(2)}) collective-permute-start(f32[131,12,2]{0,1,2:T(8,128)S(1)} %copy.39), channel_id=1, source_target_pairs={{0,1},{1,2},{2,3},{3,4},{4,5},{5,6},{6,7},{7,8},{8,9},{9,10},{10,1... | collective-permute-start | bytes 37736 | tf_op jit(solution)/shard_map/ppermute | solution.py:19
  23.1 5.3 collective-permute-start.3
  30.0 1.0 copy-start.2
  43.4 1.6 copy-start.5
  44.6 1.5 copy-start.6
  44.6 1.7 copy-start.7
  47.9 24.8 %all-to-all-start = ((f32[64,1,264]{2,1,0:T(1,128)}), f32[64,1,264]{2,1,0:T(1,128)S(1)}, u32[]{:S(2)}, u32[]{:S(2)}) async-start(f32[64,1,264]{2,1,0:T(1,128)} %reshape.63), calls=%async_computation | async-start | bytes 196608 | tf_op jit(solution)/shard_map/all_to_all | solution.py:32
  74.9 13.5 %all-to-all-start.1 = ((f32[8,1,33]{2,1,0:T(1,128)}), f32[8,1,33]{2,1,0:T(1,128)S(1)}, u32[]{:S(2)}, u32[]{:S(2)}) async-start(f32[8,1,33]{2,1,0:T(1,128)} %bitcast.11), calls=%async_computation.1 | async-start | bytes 8192 | tf_op jit(solution)/shard_map/all_to_all | solution.py:40
  89.1 9.7 %all-to-all-start.2 = ((f32[8,1,33]{2,1,0:T(1,128)}), f32[8,1,33]{2,1,0:T(1,128)S(1)}, u32[]{:S(2)}, u32[]{:S(2)}) async-start(f32[8,1,33]{2,1,0:T(1,128)} %broadcast_in_dim.54), calls=%async_computation.2 | async-start | bytes 8192 | tf_op jit(solution)/shard_map/all_to_all | solution.py:51
  99.7 17.5 %all-to-all-start.3 = ((f32[64,1,264]{2,1,0:T(1,128)}), f32[64,1,264]{2,1,0:T(1,128)S(1)}, u32[]{:S(2)}, u32[]{:S(2)}) async-start(f32[64,1,264]{2,1,0:T(1,128)} %reshape.65), calls=%async_computation.3 | async-start | bytes 196608 | tf_op jit(solution)/shard_map/all_to_all | solution.py:51
where the time goes:
time: 568 us; the launch traced here: 565 us
  local copies, waits for them, and re-layouts  232 us (41%)
  matrix products  127 us (22%)
  loops' own time  96.7 us (17%)
  starting transfers between devices  47.1 us (8%)
  waiting for transfers between devices  41.2 us (7%)
  other arithmetic  20.3 us (4%)
    dot_general x128, matrix products, row_step(): jnp.dot(masked, inverse, precision=lax.Precision.HIGHEST)  102 us
    another operation x1, loops' own time, upper_factor(): lax.fori_loop(0, extent, column_step, jnp.zeros((extent, extent), jnp.flo...  92.7 us
    dynamic_slice x128, local copies, waits for them, and re-layouts, column_step(): pivot = jnp.sqrt(lax.dynamic_slice_in_dim(column, index, 1, 0)[0])  81.4 us
    dynamic_slice x128, local copies, waits for them, and re-layouts, row_step(): pivot = lax.dynamic_slice_in_dim(row_now, index, 1, 0)[0]  75.3 us
    dynamic_update_slice x128, local copies, waits for them, and re-layouts, column_step(): return lax.dynamic_update_slice_in_dim(lower_rows, fresh[:, None], index, 1)  45.9 us
    dot_general x128, matrix products, column_step(): jnp.dot(lower_rows, row_now, precision=lax.Precision.HIGHEST)  22.1 us
    all_to_all x2, waiting for transfers between devices, from_everyone(): return lax.all_to_all(copies, axis, split_axis=0, concat_axis=0, tiled=True)  16.3 us
    all_to_all x1, starting transfers between devices, sent_and_summed(): parts = lax.all_to_all(cut_along(x, dim, devices), axis, 0, 0, tiled=True)  14.6 us
  transfers between devices with their start and end apart: 8, of which 7 were waited for; matrix products, arithmetic and copies ran while one was open for 0% of the time, Pallas kernels for 0%

commit v1 on v0

--- a/solution.py
+++ b/solution.py
@@ -1,6 +1,8 @@
 import jax
 import jax.numpy as jnp
 from jax import lax
+from jax.experimental import pallas as pl
+from jax.experimental.pallas import tpu as pltpu
 from jax.sharding import Mesh
 from jax.sharding import PartitionSpec as P
 
@@ -93,37 +95,153 @@
     )
 
 
-def upper_factor(product):
-    extent = product.shape[0]
-    places = jnp.arange(extent, dtype=jnp.int32)
-
-    def column_step(index, lower_rows):
-        row_now = lax.dynamic_slice_in_dim(lower_rows, index, 1, 0)[0]
-        column = lax.dynamic_slice_in_dim(product, index, 1, 1)[:, 0] - jnp.dot(
-            lower_rows, row_now, precision=lax.Precision.HIGHEST
-        )
-        pivot = jnp.sqrt(lax.dynamic_slice_in_dim(column, index, 1, 0)[0])
-        fresh = jnp.where(places >= index, column / pivot, jnp.float32(0.0))
-        return lax.dynamic_update_slice_in_dim(lower_rows, fresh[:, None], index, 1)
-
-    lower_rows = lax.fori_loop(0, extent, column_step, jnp.zeros((extent, extent), jnp.float32))
-    return lower_rows.T
-
-
-def upper_inverse(factor):
-    extent = factor.shape[0]
-    places = jnp.arange(extent, dtype=jnp.int32)
-
-    def row_step(count, inverse):
-        index = extent - 1 - count
-        row_now = lax.dynamic_slice_in_dim(factor, index, 1, 0)[0]
-        pivot = lax.dynamic_slice_in_dim(row_now, index, 1, 0)[0]
-        masked = jnp.where(places > index, row_now, jnp.float32(0.0))
-        unit_row = (places == index).astype(jnp.float32)
-        fresh = (unit_row - jnp.dot(masked, inverse, precision=lax.Precision.HIGHEST)) / pivot
-        return lax.dynamic_update_slice_in_dim(inverse, fresh[None, :], index, 0)
-
-    return lax.fori_loop(0, extent, row_step, jnp.zeros((extent, extent), jnp.float32))
+F32 = jnp.float32
+BF16 = jnp.bfloat16
+
+
+def lane_spread(x, lane):
+    return jnp.broadcast_to(x[:, lane : lane + 1], (8, 128))
+
+
+def row_spread(x, row):
+    return jnp.broadcast_to(x[row : row + 1, :], (8, 128))
+
+
+def split2(x):
+    hi = x.astype(BF16)
+    lo = (x - hi.astype(F32)).astype(BF16)
+    return hi, lo
+
+
+def factor_rows(x_ref, d_ref):
+    lanes = lax.broadcasted_iota(jnp.int32, (8, 128), 1)
+    rows = lax.broadcasted_iota(jnp.int32, (8, 128), 0)
+    for k in range(16):
+        base = 8 * k
+        p = x_ref[k]
+        c = [lane_spread(p, base + j) for j in range(8)]
+        a = {(i, j): row_spread(c[j], i) for j in range(8) for i in range(j, 8)}
+        in_block = (lanes >= base) & (lanes < base + 8)
+        eye = jnp.where(lanes - base == rows, F32(1.0), F32(0.0))
+        p0 = jnp.where(in_block, eye, p)
+        pb = [row_spread(p0, i) for i in range(8)]
+        inv = []
+        pivots = jnp.zeros((8, 128), F32)
+        low = {}
+        for j in range(8):
+            pivots = jnp.where(rows == j, a[j, j], pivots)
+            r = 1.0 / a[j, j]
+            inv.append(r)
+            for i in range(j + 1, 8):
+                low[i, j] = a[i, j] * r
+            for i in range(j + 1, 8):
+                for m in range(i, 8):
+                    a[m, i] = a[m, i] - a[m, j] * low[i, j]
+                pb[i] = pb[i] - low[i, j] * pb[j]
+        done = pb[0]
+        for i in range(1, 8):
+            done = jnp.where(rows == i, pb[i], done)
+        x_ref[k] = done
+        d_ref[k] = pivots
+        if k == 15:
+            break
+        q = x_ref[k + 1]
+        cq = [lane_spread(q, base + j) for j in range(8)]
+        q = jnp.where(in_block, F32(0.0), q)
+        for j in range(8):
+            mult = cq[j] * inv[j]
+            q = q - mult * pb[j]
+            for i in range(j + 1, 8):
+                cq[i] = cq[i] - mult * a[i, j]
+        x_ref[k + 1] = q
+        if k == 14:
+            continue
+        minv = {}
+        for j in range(8):
+            for i in range(j):
+                t = low[j, i]
+                for m in range(i + 1, j):
+                    t = t + low[j, m] * minv[m, i]
+                minv[j, i] = -t
+        z = []
+        scaled = [pb[j] * inv[j] for j in range(8)]
+        for i in range(8):
+            t = scaled[i]
+            for j in range(i + 1, 8):
+                t = t + minv[j, i] * scaled[j]
+            z.append(t)
+        for t in range(k + 2, 16):
+            q = x_ref[t]
+            cq = [lane_spread(q, base + j) for j in range(8)]
+            q = jnp.where(in_block, F32(0.0), q)
+            s0 = cq[0] * z[0] + cq[1] * z[1]
+            s1 = cq[2] * z[2] + cq[3] * z[3]
+            s2 = cq[4] * z[4] + cq[5] * z[5]
+            s3 = cq[6] * z[6] + cq[7] * z[7]
+            x_ref[t] = q - ((s0 + s1) + (s2 + s3))
+
+
+def tail_kernel(g_ref, d_hbm, mean_ref, out_hbm, x_ref, d_ref, dd_ref, o_ref, in_sem, out_sem):
+    fetch = pltpu.make_async_copy(d_hbm, dd_ref, in_sem)
+    fetch.start()
+    lanes = lax.broadcasted_iota(jnp.int32, (8, 128), 1)
+    rows = lax.broadcasted_iota(jnp.int32, (8, 128), 0)
+    for k in range(16):
+        x_ref[k] = g_ref[8 * k : 8 * k + 8, :] + jnp.where(lanes - 8 * k == rows, F32(1.0), F32(0.0))
+    factor_rows(x_ref, d_ref)
+    pulled = row_spread(g_ref[128:136, :], 0)
+    root = jnp.sqrt(F32(127.0))
+    shift = jnp.zeros((8, 128), F32)
+    kept = []
+    for k in range(16):
+        m = jnp.where(lanes - 8 * k <= rows, x_ref[k], F32(0.0))
+        kept.append(m)
+        y = jnp.sum(m * pulled, axis=1, keepdims=True)
+        shift = shift + m * (jnp.broadcast_to(y, (8, 128)) / d_ref[k])
+    shift = jnp.broadcast_to(jnp.sum(shift, axis=0, keepdims=True), (8, 128))
+    w = []
+    for k in range(16):
+        w.append((kept[k] / jnp.sqrt(d_ref[k]) + shift) / root)
+    w = jnp.concatenate(w, axis=0)
+    whi, wlo = split2(w)
+    both = jnp.concatenate([whi, wlo], axis=1)
+    fetch.wait()
+    for r in range(8):
+        hi, lo = split2(dd_ref[r])
+        acc = jnp.dot(both, jnp.concatenate([hi, hi], axis=0), preferred_element_type=F32)
+        acc = acc + jnp.dot(both, jnp.concatenate([lo, lo], axis=0), preferred_element_type=F32)
+        acc = acc + mean_ref[r : r + 1, :]
+        o_ref[0, pl.ds(r, 128, stride=8), :] = acc[:, 0:128]
+        o_ref[1, pl.ds(r, 128, stride=8), :] = acc[:, 128:256]
+    outs = [
+        pltpu.make_async_copy(o_ref.at[n], out_hbm.at[:, pl.ds(128 * n, 128)], out_sem.at[n]) for n in range(2)
+    ]
+    for c in outs:
+        c.start()
+    for c in outs:
+        c.wait()
+
+
+def tail(g, departures, mean):
+    return pl.pallas_call(
+        tail_kernel,
+        out_shape=jax.ShapeDtypeStruct((1024, 256), F32),
+        in_specs=[
+            pl.BlockSpec(memory_space=pltpu.VMEM),
+            pl.BlockSpec(memory_space=pl.ANY),
+            pl.BlockSpec(memory_space=pltpu.VMEM),
+        ],
+        out_specs=pl.BlockSpec(memory_space=pl.ANY),
+        scratch_shapes=[
+            pltpu.VMEM((16, 8, 128), F32),
+            pltpu.VMEM((16, 8, 128), F32),
+            pltpu.VMEM((8, 128, 256), F32),
+            pltpu.VMEM((2, 1024, 128), F32),
+            pltpu.SemaphoreType.DMA,
+            pltpu.SemaphoreType.DMA((2,)),
+        ],
+        name="tail",
+    )(g, departures, mean)
 
 
 def body(
@@ -152,17 +270,12 @@
     root = jnp.sqrt(jnp.float32(sample_total - 1))
     scaled = (measurement_vector - obs_mean) / (obs_error * root)
     innovation = (obs_value - obs_mean) / obs_error
-    eye = jnp.eye(sample_total, dtype=jnp.float32)
     pull_part = jnp.dot(scaled, innovation[:, None], precision=lax.Precision.HIGHEST)
     gram_part = jnp.dot(scaled, scaled.T, precision=lax.Precision.HIGHEST)
     gram_total, pulled = together((gram_part, pull_part), ("row_0", ("row_1", "col_0", "col_1")))
-    factor = upper_factor(eye + gram_total)
-    inverse = upper_inverse(factor)
-    middle = jnp.dot(inverse.T, pulled, precision=lax.Precision.HIGHEST)
-    shift = jnp.dot(inverse, middle, precision=lax.Precision.HIGHEST)
-    weights = (shift + inverse) / root
-    assimilate_measurements = jnp.dot(weights.T, sample_departures, precision=lax.Precision.HIGHEST)
-    return sample_centroid + assimilate_measurements.reshape(predicted_fields.shape)
+    g = jnp.concatenate([gram_total, jnp.pad(pulled.T, ((0, 7), (0, 0)))], axis=0)
+    departures = jnp.swapaxes(sample_departures.reshape(128, 8, 256), 0, 1)
+    return tail(g, departures, sample_centroid).reshape(128, 8, 256)
 
 
 def solution(mesh):

time: 568 us -> 116 us (0.20)
  local copies, waits for them, and re-layouts: 232 us -> 7.68 us
  matrix products: 127 us -> 1.47 us
  loops' own time: 96.7 us -> 0 us
  blocking collectives: 0 us -> 38 us
  starting transfers between devices: 47.1 us -> 25.1 us
  waiting for transfers between devices: 41.2 us -> 24.4 us
  other arithmetic: 20.3 us -> 10.3 us
  Pallas kernels: 0 us -> 7.89 us
    dynamic_slice x256 -> x0, local copies, waits for them, and re-layouts: 157 us -> none  [the longest x128 81.4 us: column_step(): pivot = jnp.sqrt(lax.dynamic_slice_in_dim(column, index, 1, 0)[0])]
    dot_general x259 -> x0, matrix products: 126 us -> none  [the longest x128 102 us: row_step(): jnp.dot(masked, inverse, precision=lax.Precision.HIGHEST)]
    another operation x2 -> x0, loops' own time: 96.7 us -> none  [the longest x1 92.7 us: upper_factor(): lax.fori_loop(0, extent, column_step, jnp.zeros((extent, extent), jnp.flo...]
    dynamic_update_slice x256 -> x0, local copies, waits for them, and re-layouts: 49.9 us -> none  [the longest x128 45.9 us: column_step(): return lax.dynamic_update_slice_in_dim(lower_rows, fresh[:, None], index, 1)]
    all_to_all x0 -> x2, blocking collectives: none -> 38 us  [the longest x1 24.6 us: sent_and_summed(): parts = lax.all_to_all(cut_along(x, dim, devices), axis, 0, 0, tiled=True)]
    all_to_all x2 -> x0, starting transfers between devices: 21.7 us -> none  [the longest x1 14.6 us: sent_and_summed(): parts = lax.all_to_all(cut_along(x, dim, devices), axis, 0, 0, tiled=True)]
    all_to_all x2 -> x0, waiting for transfers between devices: 16.7 us -> none  [the longest x1 10.2 us: sent_and_summed(): parts = lax.all_to_all(cut_along(x, dim, devices), axis, 0, 0, tiled=True)]
    broadcast_in_dim x128 -> x1, local copies, waits for them, and re-layouts: 14.5 us -> 0.01 us  [body(): spreading_coefficient[None]]
  transfers between devices with their start and end apart: 8 -> 6, of which waited for: 7 -> 5; matrix products, arithmetic and copies ran while one was open for 0% -> 2% of each run, Pallas kernels for 0% -> 0%
where the time goes in v1:
time: 116 us; the launch traced here: 115 us
  blocking collectives  38 us (33%)
  starting transfers between devices  25.1 us (22%)
  waiting for transfers between devices  24.4 us (21%)
  other arithmetic  10.3 us (9%)
  Pallas kernels  7.89 us (7%)
  local copies, waits for them, and re-layouts  7.68 us (7%)
  matrix products  1.47 us (1%)
    all_to_all x1, blocking collectives, sent_and_summed(): parts = lax.all_to_all(cut_along(x, dim, devices), axis, 0, 0, tiled=True)  24.6 us
    all_to_all x2, waiting for transfers between devices, from_everyone(): return lax.all_to_all(copies, axis, split_axis=0, concat_axis=0, tiled=True)  15.6 us
    all_to_all x1, blocking collectives, summed_rows(): lax.all_to_all(nearer, far, split_axis=0, concat_axis=0, tiled=True)  13.4 us
    ppermute x2, starting transfers between devices, with_halo(): before = lax.ppermute(last, axis, up)  11.5 us
    all_to_all x2, starting transfers between devices, from_everyone(): return lax.all_to_all(copies, axis, split_axis=0, concat_axis=0, tiled=True)  10.3 us
    pallas_call x1, Pallas kernels, tail(): pl.pallas_call(tail_kernel, out_shape=jax.ShapeDtypeStruct((1024, 256), F...  7.89 us
    ppermute x2, waiting for transfers between devices, with_halo(): after = lax.ppermute(first, axis, down)  6.68 us
    sub x1, other arithmetic, propagate_dynamics(): centre + spreading_coefficient * spread  3.88 us
  transfers between devices with their start and end apart: 6, of which 5 were waited for; matrix products, arithmetic and copies ran while one was open for 2% of the time, Pallas kernels for 0%

profile of v1, /device:TPU:1, one launch (start us, length us, event | category | flops | bytes accessed | tf_op | source)
XLA Modules:
  0.0 115.3 jit_solution(6597014511939940604)
XLA Ops:
  0.0 1.6 %copy.12 = f32[128,8,256]{2,0,1:T(8,128)S(1)} copy(f32[128,8,256]{2,1,0:T(8,128)} %param.6) | data formatting | bytes 2097152 | tf_op args[0]
  1.7 4.0 %collective-permute-start = (f32[131,2,256]{2,0,1:T(8,128)S(1)}, f32[131,2,256]{2,0,1:T(8,128)S(1)}, u32[]{:S(2)}, u32[]{:S(2)}) collective-permute-start(f32[131,2,256]{2,0,1:T(8,128)S(1)} %get-tuple-element.11), channel_id=1, source_target_pairs={{0,16},{16,32},{32,48},{48,64},{64,80},{80,96},{96,112},{112,128},... | collective-permute-start | bytes 804872 | tf_op jit(solution)/shard_map/ppermute | solution.py:21
  5.7 1.3 %collective-permute-start.1 = (f32[131,2,256]{2,0,1:T(8,128)S(1)}, f32[131,2,256]{2,0,1:T(8,128)S(1)}, u32[]{:S(2)}, u32[]{:S(2)}) collective-permute-start(f32[131,2,256]{2,0,1:T(8,128)S(1)} %get-tuple-element.12), channel_id=1, source_target_pairs={{16,0},{32,16},{48,32},{64,48},{80,64},{96,80},{112,96},{128,112},... | collective-permute-start | bytes 804872 | tf_op jit(solution)/shard_map/ppermute | solution.py:22
  7.0 2.1 %collective-permute-done = f32[131,2,256]{2,0,1:T(8,128)S(1)} collective-permute-done((f32[131,2,256]{2,0,1:T(8,128)S(1)}, f32[131,2,256]{2,0,1:T(8,128)S(1)}, u32[]{:S(2)}, u32[]{:S(2)}) %collective-permute-start) | collective-permute-done | bytes 268320 | tf_op jit(solution)/shard_map/ppermute | solution.py:21
  9.1 3.8 %collective-permute-done.1 = f32[131,2,256]{2,0,1:T(8,128)S(1)} collective-permute-done((f32[131,2,256]{2,0,1:T(8,128)S(1)}, f32[131,2,256]{2,0,1:T(8,128)S(1)}, u32[]{:S(2)}, u32[]{:S(2)}) %collective-permute-start.1) | collective-permute-done | bytes 268320 | tf_op jit(solution)/shard_map/ppermute | solution.py:22
  13.9 7.6 %collective-permute-start.2 = (f32[131,12,2]{0,2,1:T(2,128)S(1)}, f32[131,12,2]{0,2,1:T(2,128)S(1)}, u32[]{:S(2)}, u32[]{:S(2)}) collective-permute-start(f32[131,12,2]{0,2,1:T(2,128)S(1)} %copy.14), channel_id=1, source_target_pairs={{0,1},{1,2},{2,3},{3,4},{4,5},{5,6},{6,7},{7,8},{8,9},{9,10},{10,1... | collective-permute-start | bytes 37736 | tf_op jit(solution)/shard_map/ppermute | solution.py:21
  21.9 1.9 %collective-permute-start.3 = (f32[131,12,2]{0,2,1:T(2,128)S(1)}, f32[131,12,2]{0,2,1:T(2,128)S(1)}, u32[]{:S(2)}, u32[]{:S(2)}) collective-permute-start(f32[131,12,2]{0,2,1:T(2,128)S(1)} %copy.15), channel_id=1, source_target_pairs={{1,0},{2,1},{3,2},{4,3},{5,4},{6,5},{7,6},{8,7},{9,8},{10,9},{11,1... | collective-permute-start | bytes 37736 | tf_op jit(solution)/shard_map/ppermute | solution.py:22
  24.2 2.8 %collective-permute-done.3 = f32[131,12,2]{0,2,1:T(2,128)S(1)} collective-permute-done((f32[131,12,2]{0,2,1:T(2,128)S(1)}, f32[131,12,2]{0,2,1:T(2,128)S(1)}, u32[]{:S(2)}, u32[]{:S(2)}) %collective-permute-start.3) | collective-permute-done | bytes 12608 | tf_op jit(solution)/shard_map/ppermute | solution.py:22
  27.8 1.0 pad_maximum_fusion
  28.8 3.9 %fusion.5 = f32[128,10,258]{2,0,1:T(8,128)S(1)} fusion(f32[131,12,2]{2,0,1:T(8,128)S(1)} %copy.17, f32[131,2,256]{2,0,1:T(8,128)S(1)} %collective-permute-done.1, f32[131,2,256]{2,0,1:T(8,128)S(1)} %collective-permute-done, f32[2,8,256]{2,0,1:T(2,128)S(1)} %copy.13, f32[1,8,256]{2,0,1:T(1,128)S(1)} %broadcast_in_dim.6, f32[128,8,256]{2,0,1:T(8,128)S(1)} %copy.12, ...), kind=kLoop, calls=%fused_computation.8 | loop fusion | flops 7595520 | bytes 6949680 | tf_op jit(solution)/shard_map/sub | solution.py:91
  32.7 1.2 %fusion.16 = (f32[8,256]{1,0:T(8,128)S(1)}, f32[128,8,256]{2,0,1:T(8,128)S(1)}) fusion(f32[8,256]{1,0:T(8,128)S(1)} %get-tuple-element.14, f32[8,256]{1,0:T(8,128)S(1)} %get-tuple-element.13, f32[128,10,258]{2,0,1:T(8,128)S(1)} %fusion.5, f32[8,256]{1,0:T(8,128)S(1)} %copy-done.2), kind=kLoop, calls=%fused_computation.56 | loop fusion | flops 3667968 | bytes 6324224 | tf_op jit(solution)/shard_map/reduce_sum | solution.py:267
  34.5 1.0 fusion.19
  36.7 24.6 %all_to_all.28 = f32[64,1,264]{2,1,0:T(1,128)S(1)} all-to-all(f32[64,1,264]{2,1,0:T(1,128)S(1)} %reshape.45), channel_id=1, replica_groups=mesh['row_0'=8,'row_1'=4,'col_0'=8,'col_1'=2] {'row_1','col_0','col_1'}, dimensions={0} | all-to-all | bytes 135168 | tf_op jit(solution)/shard_map/all_to_all | solution.py:34
  61.9 0.9 reduce.1
  63.1 13.4 %all_to_all.29 = f32[8,1,33]{2,1,0:T(1,128)S(1)} all-to-all(f32[8,1,33]{2,1,0:T(1,128)S(1)} %bitcast.34), channel_id=1, replica_groups=mesh['row_0'=8,'row_1'=4,'col_0'=8,'col_1'=2] {'row_0'}, dimensions={0} | all-to-all | bytes 2112 | tf_op jit(solution)/shard_map/all_to_all | solution.py:42
  77.1 3.3 %all-to-all-start.2 = ((f32[8,1,33]{2,1,0:T(1,128)}), f32[8,1,33]{2,1,0:T(1,128)S(1)}, u32[]{:S(2)}, u32[]{:S(2)}) async-start(f32[8,1,33]{2,1,0:T(1,128)} %broadcast_in_dim.7), calls=%async_computation.2 | async-start | bytes 8192 | tf_op jit(solution)/shard_map/all_to_all | solution.py:53
  80.4 6.4 %all-to-all-done.2 = f32[8,1,33]{2,1,0:T(1,128)S(1)} async-done(((f32[8,1,33]{2,1,0:T(1,128)}), f32[8,1,33]{2,1,0:T(1,128)S(1)}, u32[]{:S(2)}, u32[]{:S(2)}) %all-to-all-start.2) | async-done | bytes 1088 | tf_op jit(solution)/shard_map/all_to_all | solution.py:53
  86.8 0.9 reshape.47
  87.7 7.0 %all-to-all-start.3 = ((f32[64,1,264]{2,1,0:T(1,128)}), f32[64,1,264]{2,1,0:T(1,128)S(1)}, u32[]{:S(2)}, u32[]{:S(2)}) async-start(f32[64,1,264]{2,1,0:T(1,128)} %reshape.47), calls=%async_computation.3 | async-start | bytes 196608 | tf_op jit(solution)/shard_map/all_to_all | solution.py:53
  94.7 1.1 subtract_bitcast_fusion.d_hbm
  95.8 9.2 %all-to-all-done.3 = f32[64,1,264]{2,1,0:T(1,128)S(1)} async-done(((f32[64,1,264]{2,1,0:T(1,128)}), f32[64,1,264]{2,1,0:T(1,128)S(1)}, u32[]{:S(2)}, u32[]{:S(2)}) %all-to-all-start.3) | async-done | bytes 67616 | tf_op jit(solution)/shard_map/all_to_all | solution.py:53
  105.0 0.9 reduce.2
  106.6 0.6 select_maximum_fusion.g_ref
  107.2 7.9 %tail.1 = f32[1024,256]{1,0:T(8,128)} custom-call(f32[136,128]{1,0:T(8,128)} %select_maximum_fusion.g_ref, f32[8,128,256]{2,1,0:T(8,128)} %subtract_bitcast_fusion.d_hbm, f32[8,256]{1,0:T(8,128)} %copy-done), custom_call_target="tpu_custom_call" | custom-call | tf_op jit(solution)/shard_map/tail/pallas_call | solution.py:226
  (49 shorter events, 6.4 us)
Async XLA Ops:
  0.0 1.6 %copy-start.1 = (f32[2,8,256]{2,1,0:T(8,128)S(1)}, f32[2,8,256]{2,1,0:T(8,128)}, u32[]{:S(2)}) copy-start(f32[2,8,256]{2,1,0:T(8,128)} %param.8) | copy-start | bytes 49156
  0.0 1.6 %copy-start.2 = (f32[8,256]{1,0:T(8,128)S(1)}, f32[8,256]{1,0:T(8,128)}, u32[]{:S(2)}) copy-start(f32[8,256]{1,0:T(8,128)} %param.7) | copy-start | bytes 24580
  1.7 7.4 %collective-permute-start = (f32[131,2,256]{2,0,1:T(8,128)S(1)}, f32[131,2,256]{2,0,1:T(8,128)S(1)}, u32[]{:S(2)}, u32[]{:S(2)}) collective-permute-start(f32[131,2,256]{2,0,1:T(8,128)S(1)} %get-tuple-element.11), channel_id=1, source_target_pairs={{0,16},{16,32},{32,48},{48,64},{64,80},{80,96},{96,112},{112,128},... | collective-permute-start | bytes 804872 | tf_op jit(solution)/shard_map/ppermute | solution.py:21
  5.7 7.3 %collective-permute-start.1 = (f32[131,2,256]{2,0,1:T(8,128)S(1)}, f32[131,2,256]{2,0,1:T(8,128)S(1)}, u32[]{:S(2)}, u32[]{:S(2)}) collective-permute-start(f32[131,2,256]{2,0,1:T(8,128)S(1)} %get-tuple-element.12), channel_id=1, source_target_pairs={{16,0},{32,16},{48,32},{64,48},{80,64},{96,80},{112,96},{128,112},... | collective-permute-start | bytes 804872 | tf_op jit(solution)/shard_map/ppermute | solution.py:22
  13.1 10.7 %copy-start.4 = (f32[128]{0:T(128)S(1)}, f32[128]{0:T(128)}, u32[]{:S(2)}) copy-start(f32[128]{0:T(128)} %param.11) | copy-start | bytes 1540
  13.9 10.0 %collective-permute-start.2 = (f32[131,12,2]{0,2,1:T(2,128)S(1)}, f32[131,12,2]{0,2,1:T(2,128)S(1)}, u32[]{:S(2)}, u32[]{:S(2)}) collective-permute-start(f32[131,12,2]{0,2,1:T(2,128)S(1)} %copy.14), channel_id=1, source_target_pairs={{0,1},{1,2},{2,3},{3,4},{4,5},{5,6},{6,7},{7,8},{8,9},{9,10},{10,1... | collective-permute-start | bytes 37736 | tf_op jit(solution)/shard_map/ppermute | solution.py:21
  21.9 5.1 %collective-permute-start.3 = (f32[131,12,2]{0,2,1:T(2,128)S(1)}, f32[131,12,2]{0,2,1:T(2,128)S(1)}, u32[]{:S(2)}, u32[]{:S(2)}) collective-permute-start(f32[131,12,2]{0,2,1:T(2,128)S(1)} %copy.15), channel_id=1, source_target_pairs={{1,0},{2,1},{3,2},{4,3},{5,4},{6,5},{7,6},{8,7},{9,8},{10,9},{11,1... | collective-permute-start | bytes 37736 | tf_op jit(solution)/shard_map/ppermute | solution.py:22
  33.8 0.7 copy-start.3
  33.9 1.9 %copy-start.5 = (f32[128]{0:T(128)S(1)}, f32[128]{0:T(128)}, u32[]{:S(2)}) copy-start(f32[128]{0:T(128)} %param.10) | copy-start | bytes 1540
  77.1 9.7 %all-to-all-start.2 = ((f32[8,1,33]{2,1,0:T(1,128)}), f32[8,1,33]{2,1,0:T(1,128)S(1)}, u32[]{:S(2)}, u32[]{:S(2)}) async-start(f32[8,1,33]{2,1,0:T(1,128)} %broadcast_in_dim.7), calls=%async_computation.2 | async-start | bytes 8192 | tf_op jit(solution)/shard_map/all_to_all | solution.py:53
  80.4 25.8 %copy-start = (f32[8,256]{1,0:T(8,128)}, f32[8,256]{1,0:T(8,128)S(1)}, u32[]{:S(2)}) copy-start(f32[8,256]{1,0:T(8,128)S(1)} %broadcast_multiply_fusion.mean_ref) | copy-start | bytes 24580
  87.7 17.3 %all-to-all-start.3 = ((f32[64,1,264]{2,1,0:T(1,128)}), f32[64,1,264]{2,1,0:T(1,128)S(1)}, u32[]{:S(2)}, u32[]{:S(2)}) async-start(f32[64,1,264]{2,1,0:T(1,128)} %reshape.47), calls=%async_computation.3 | async-start | bytes 196608 | tf_op jit(solution)/shard_map/all_to_all | solution.py:53

commit v2 on v1

--- a/solution.py
+++ b/solution.py
@@ -9,92 +9,6 @@
 ROW_COL = ("row_0", "row_1", "col_0", "col_1")
 ROW = ("row_0", "row_1")
 COL = ("col_0", "col_1")
-
-
-def with_halo(x, sides, width):
-    for axis, dim in sides:
-        devices, length = (lax.axis_size(axis), x.shape[dim])
-        up = [(i, (i + 1) % devices) for i in range(devices - 1)]
-        down = [(j, i) for i, j in up]
-        last = lax.slice_in_dim(x, length - width, length, axis=dim)
-        first = lax.slice_in_dim(x, 0, width, axis=dim)
-        before = lax.ppermute(last, axis, up)
-        after = lax.ppermute(first, axis, down)
-        x = jnp.concatenate([before, x, after], axis=dim)
-    return x
-
-
-def cut_along(x, dim, devices):
-    before, after = (x.shape[:dim], x.shape[dim + 1 :])
-    return jnp.moveaxis(x.reshape(*before, devices, -1, *after), dim, 0)
-
-
-def sent_and_summed(x, axis, dim):
-    devices = lax.axis_size(axis)
-    parts = lax.all_to_all(cut_along(x, dim, devices), axis, 0, 0, tiled=True)
-    return jnp.sum(parts, axis=0)
-
-
-def summed_rows(x, axes, dim):
-    far, near = axes
-    parts = cut_along(x, dim, lax.axis_size(far))
-    nearer = sent_and_summed(parts, near, dim + 1)
-    arrived = lax.all_to_all(nearer, far, split_axis=0, concat_axis=0, tiled=True)
-    return arrived.sum(axis=0)
-
-
-def rows_for(lines, devices):
-    spare = -len(lines) % devices
-    return jnp.pad(lines, [(0, spare)] + [(0, 0)] * (lines.ndim - 1))
-
-
-def from_everyone(x, axis):
-    copies = jnp.broadcast_to(x, (lax.axis_size(axis), *x.shape))
-    return lax.all_to_all(copies, axis, split_axis=0, concat_axis=0, tiled=True)
-
-
-def laid_out(parts, dim):
-    lengths = list(parts.shape[1:])
-    lengths[dim] *= parts.shape[0]
-    return jnp.moveaxis(parts, 0, dim).reshape(lengths)
-
-
-def gather_axes(x, axes, dim):
-    far, near = axes
-    first = from_everyone(x, far)
-    parts = jnp.swapaxes(from_everyone(first, near), 0, 1)
-    return laid_out(parts.reshape(-1, *x.shape), dim)
-
-
-def sum_by_parts(x, axes):
-    own = summed_rows(rows_for(x, lax.axis_size(axes[0]) * lax.axis_size(axes[1])), axes, 0)
-    whole = gather_axes(own, axes, 0)
-    return whole[: len(x)].reshape(x.shape)
-
-
-def together(arrays, axis):
-    ends = [0]
-    for a in arrays:
-        ends.append(ends[-1] + a.size)
-    running = sum_by_parts(jnp.concatenate([a.ravel() for a in arrays]), axis)
-    return tuple((running[b:e].reshape(a.shape) for a, b, e in zip(arrays, ends, ends[1:])))
-
-
-def propagate_dynamics(padded, spreading_coefficient, transport_courant):
-    centre = padded[:, 1:-1, 1:-1]
-    upper = padded[:, :-2, 1:-1]
-    lower = padded[:, 2:, 1:-1]
-    left_side = padded[:, 1:-1, :-2]
-    right_side = padded[:, 1:-1, 2:]
-    spread = upper + lower + left_side + right_side - 4.0 * centre
-    return (
-        centre
-        + spreading_coefficient * spread
-        - transport_courant[0] * (centre - upper)
-        - transport_courant[1] * (centre - left_side)
-    )
-
-
 F32 = jnp.float32
 BF16 = jnp.bfloat16
 
@@ -186,10 +100,22 @@
     fetch.start()
     lanes = lax.broadcasted_iota(jnp.int32, (8, 128), 1)
     rows = lax.broadcasted_iota(jnp.int32, (8, 128), 0)
+    upper = g_ref[0:64, :]
+    lanes64 = lax.broadcasted_iota(jnp.int32, (64, 128), 1)
+    rows64 = lax.broadcasted_iota(jnp.int32, (64, 128), 0)
+    half = jnp.concatenate(
+        [
+            jnp.where((lanes64 >= 64) | (lanes64 < rows64), upper, F32(0.0)),
+            jnp.where(lanes64 - 64 > rows64, pltpu.roll(upper, 64, 1), F32(0.0)),
+        ],
+        axis=0,
+    )
+    gram = half + half.T
+    diagonal = row_spread(g_ref[64:72, :], 1) + F32(1.0)
     for k in range(16):
-        x_ref[k] = g_ref[8 * k : 8 * k + 8, :] + jnp.where(lanes - 8 * k == rows, F32(1.0), F32(0.0))
+        x_ref[k] = jnp.where(lanes - 8 * k == rows, diagonal, gram[8 * k : 8 * k + 8])
     factor_rows(x_ref, d_ref)
-    pulled = row_spread(g_ref[128:136, :], 0)
+    pulled = row_spread(g_ref[64:72, :], 0)
     root = jnp.sqrt(F32(127.0))
     shift = jnp.zeros((8, 128), F32)
     kept = []
@@ -244,38 +170,368 @@
     )(g, departures, mean)
 
 
+MESH_IDS = pl.DeviceIdType.MESH
+HIGHEST = lax.Precision.HIGHEST
+CHUNKS = 4
+PART = 128 // CHUNKS
+
+
+def send(src, dst, sems, slot, device, landed=None):
+    landed = slot if landed is None else landed
+    return pltpu.make_async_remote_copy(
+        src_ref=src,
+        dst_ref=dst,
+        send_sem=sems[0].at[slot],
+        recv_sem=sems[1].at[landed],
+        device_id=device,
+        device_id_type=MESH_IDS,
+    )
+
+
+def stencil(get, coef_ref, row, tiles, lanes):
+    centre = [get(t, row) for t in range(3)]
+    right_of = [pltpu.roll(v, 127, 1) for v in centre]
+    left_of = [pltpu.roll(v, 1, 1) for v in centre]
+    out = []
+    for t in tiles:
+        left = jnp.where(lanes == 0, left_of[(t + 2) % 3], left_of[t])
+        right = jnp.where(lanes == 127, right_of[(t + 1) % 3], right_of[t])
+        w = [coef_ref[n, t, row : row + 1, :] for n in range(5)]
+        out.append(
+            (w[0] * centre[t] + w[1] * get(t, row - 1)) + (w[2] * get(t, row + 1) + (w[3] * left + w[4] * right))
+        )
+    return out
+
+
+def front_kernel(
+    prior_hbm, spread_ref, courant_ref, cells_ref, value_ref, error_ref,
+    d_hbm, mean_ref, total_ref,
+    nat_ref, u_ref, f_ref, full_ref, d_ref, pick_ref, raw_ref, coef_ref,
+    edge_ref, colin_ref, rowc_ref, rowin_ref, cor_ref, comb_ref, acc_ref,
+    part_ref, rs_ref, ysrc_ref, yin_ref, zsrc_ref, zin_ref, fin_ref, gat_ref,
+    load_sem, store_sem, halo_s, halo_r, small_s, small_r, rs_s, rs_r, y_s, y_r, z_s, z_r, ag_s, ag_r,
+):
+    y, x = lax.axis_index("row_0"), lax.axis_index("row_1")
+    z, core = lax.axis_index("col_0"), lax.axis_index("col_1")
+    row, col = y * 4 + x, z * 2 + core
+
+    def at_row(n):
+        n = lax.rem(n + 32, 32)
+        return (n // 4, lax.rem(n, 4), z, core)
+
+    def at_col(n):
+        n = lax.rem(n + 16, 16)
+        return (y, x, n // 2, lax.rem(n, 2))
+
+    up, down, left, right = at_row(row - 1), at_row(row + 1), at_col(col - 1), at_col(col + 1)
+    me = x * 2 + core
+    group = [lax.rem(me + i, 8) for i in range(1, 8)]
+    group_dev = [(y, g // 2, z, lax.rem(g, 2)) for g in group]
+    ys = [lax.rem(y + i, 8) for i in range(1, 8)]
+    zs = [lax.rem(z + i, 8) for i in range(1, 8)]
+    y_dev = [(n, x, z, core) for n in ys]
+    z_dev = [(y, x, n, core) for n in zs]
+
+    barrier = pltpu.get_barrier_semaphore()
+    everyone = [up, down, left, right] + group_dev + y_dev + z_dev
+    for device in everyone:
+        pl.semaphore_signal(barrier, inc=1, device_id=device, device_id_type=MESH_IDS)
+
+    loads = [
+        pltpu.make_async_copy(prior_hbm.at[:, pl.ds(128 * t, 128)], nat_ref.at[t], load_sem.at[t]) for t in range(2)
+    ]
+    for c in loads:
+        c.start()
+
+    lanes8 = lax.broadcasted_iota(jnp.int32, (8, 128), 1)
+    for t in range(2):
+        cut = slice(128 * t, 128 * t + 128)
+        for n, block in enumerate((spread_ref[:, cut], courant_ref[0:8, cut], courant_ref[8:16, cut])):
+            raw_ref[n, t, 1:9, :] = block
+            rowc_ref[t, n : n + 1, :] = block[7:8, :]
+            rowc_ref[t, n + 3 : n + 4, :] = block[0:1, :]
+        rowc_ref[t, 6:8, :] = jnp.zeros((2, 128), F32)
+    edge = jnp.zeros((8, 128), F32)
+    for n in range(3):
+        last = spread_ref[:, 128:256] if n == 0 else courant_ref[8 * n - 8 : 8 * n, 128:256]
+        first = spread_ref[:, 0:128] if n == 0 else courant_ref[8 * n - 8 : 8 * n, 0:128]
+        edge = jnp.where(lanes8 == n, pltpu.roll(last, 1 + n, 1), edge)
+        edge = jnp.where(lanes8 == n + 3, pltpu.roll(first, 3 + n, 1), edge)
+    edge_ref[0, 16:24, :] = edge
+    edge_ref[1, 16:24, :] = edge
+
+    for c in loads:
+        c.wait()
+    for r in (0, 1, 6, 7, 2, 3, 4, 5):
+        for t in range(2):
+            u_ref[t, 2 + r] = nat_ref[t, pl.ds(r, 128, stride=8), :]
+    pl.semaphore_wait(barrier, len(everyone))
+
+    halo = []
+    for part in range(CHUNKS):
+        some = pl.ds(part * PART, PART)
+        for t in range(2):
+            slot = part * 4 + t * 2
+            halo.append(send(u_ref.at[t, 2:4, some, :], u_ref.at[t, 10:12, some, :], (halo_s, halo_r), slot, up))
+            halo.append(send(u_ref.at[t, 8:10, some, :], u_ref.at[t, 0:2, some, :], (halo_s, halo_r), slot + 1, down))
+    small = (small_s, small_r)
+    rows_out = [send(rowc_ref, rowin_ref.at[1], small, 0, up), send(rowc_ref, rowin_ref.at[0], small, 1, down)]
+    for c in rows_out:
+        c.start()
+    for c in halo[:4]:
+        c.start()
+
+    lanes = lax.broadcasted_iota(jnp.int32, (128, 128), 1)
+    ends = jnp.zeros((128, 128), F32)
+    for r in range(8):
+        ends = jnp.where((lanes >> 1) == r, pltpu.roll(u_ref[1, 2 + r], 2 + 2 * r, 1), ends)
+        ends = jnp.where((lanes >> 1) == r + 8, pltpu.roll(u_ref[0, 2 + r], 16 + 2 * r, 1), ends)
+    ends = ends.T
+    edge_ref[0, 0:16, :] = ends[0:16]
+    edge_ref[1, 0:16, :] = ends[16:32]
+    cols_out = [
+        send(edge_ref.at[0], colin_ref.at[0], small, 2, right),
+        send(edge_ref.at[1], colin_ref.at[1], small, 3, left),
+    ]
+    for c in cols_out:
+        c.start()
+    for c in halo[4:]:
+        c.start()
+
+    cells = cells_ref[...]
+    places = lax.broadcasted_iota(jnp.int32, (256, 128), 0)
+    for r in range(8):
+        pick_ref[r] = jnp.where(places + 256 * r == cells, F32(1.0), F32(0.0)).astype(BF16)
+
+    for c in cols_out:
+        c.wait()
+    corners_out = [
+        send(colin_ref.at[:, 8:16, :], cor_ref.at[0], small, 4, down),
+        send(colin_ref.at[:, 0:8, :], cor_ref.at[1], small, 5, up),
+    ]
+    for c in corners_out:
+        c.start()
+    for c in rows_out:
+        c.wait()
+
+    for n in range(3):
+        for t in range(2):
+            raw_ref[n, t, 0:1, :] = rowin_ref[0, t, n : n + 1, :]
+            raw_ref[n, t, 9:10, :] = rowin_ref[1, t, n + 3 : n + 4, :]
+        beyond = jnp.where(
+            lanes8 == 127,
+            pltpu.roll(colin_ref[0, 16:24, :], 127 - n, 1),
+            pltpu.roll(colin_ref[1, 16:24, :], 125 - n, 1),
+        )
+        raw_ref[n, 2, 0:1, :] = jnp.zeros((1, 128), F32)
+        raw_ref[n, 2, 1:9, :] = jnp.where((lanes8 == 127) | (lanes8 == 0), beyond, F32(0.0))
+        raw_ref[n, 2, 9:10, :] = jnp.zeros((1, 128), F32)
+    wide = lax.broadcasted_iota(jnp.int32, (10, 128), 1)
+    deep = lax.broadcasted_iota(jnp.int32, (10, 128), 0)
+    for t in range(3):
+        k, t0, t1 = (raw_ref[n, t, 0:10, :] for n in range(3))
+        zero = jnp.zeros_like(k)
+        coef_ref[0, t, 0:10, :] = 1.0 - 4.0 * k - t0 - t1
+        coef_ref[1, t, 0:10, :] = jnp.where((deep == 1) & (row == 0), zero, k + t0)
+        coef_ref[2, t, 0:10, :] = jnp.where((deep == 8) & (row == 31), zero, k)
+        w_left, w_right = k + t1, k
+        if t == 0:
+            w_left = jnp.where((wide == 0) & (col == 0), zero, w_left)
+        if t == 1:
+            w_right = jnp.where((wide == 127) & (col == 15), zero, w_right)
+        coef_ref[3, t, 0:10, :] = w_left
+        coef_ref[4, t, 0:10, :] = w_right
+
+    comb_ref[...] = jnp.zeros((128, 128), F32)
+    for r in range(8):
+        comb_ref[4 * r + 4 : 4 * r + 6, :] = colin_ref[0, 2 * r : 2 * r + 2, :]
+        comb_ref[4 * r + 6 : 4 * r + 8, :] = colin_ref[1, 2 * r : 2 * r + 2, :]
+    for c in corners_out:
+        c.wait()
+    for side in range(2):
+        comb_ref[2 * side : 2 * side + 2, :] = cor_ref[0, side, 6:8, :]
+        comb_ref[36 + 2 * side : 38 + 2 * side, :] = cor_ref[1, side, 0:2, :]
+    turned = comb_ref[...].T
+    for n in range(10):
+        u_ref[2, n + 1] = pltpu.roll(turned, (126 - 4 * n) % 128, 1)
+
+    few = lax.broadcasted_iota(jnp.int32, (PART, 128), 1)
+
+    def first_step(some, n):
+        tiles = range(3) if 1 <= n <= 8 else range(2)
+        for t, v in zip(tiles, stencil(lambda t, i: u_ref[t, i + 1, some, :], coef_ref, n, tiles, few)):
+            f_ref[t, n, some, :] = v
+
+    def second_step(some, n):
+        for t, v in zip(range(2), stencil(lambda t, i: f_ref[t, i, some, :], coef_ref, n, range(2), few)):
+            full_ref[n - 1, some, 128 * t : 128 * t + 128] = v
+
+    @pl.loop(0, CHUNKS)
+    def _(part):
+        some = pl.ds(pl.multiple_of(part * PART, PART), PART)
+        for n in range(2, 8):
+            first_step(some, n)
+        for n in range(3, 7):
+            second_step(some, n)
+
+    def observe(n):
+        v = full_ref[n]
+        hi = v.astype(BF16)
+        rest = v - hi.astype(F32)
+        mid = rest.astype(BF16)
+        lo = (rest - mid.astype(F32)).astype(BF16)
+        return jnp.dot(jnp.concatenate([hi, mid, lo], axis=0), pick_ref[n], preferred_element_type=F32)
+
+    acc_ref[...] = (observe(2) + observe(3)) + (observe(4) + observe(5))
+
+    for part in range(CHUNKS):
+        some = slice(part * PART, part * PART + PART)
+        for c in halo[4 * part : 4 * part + 4]:
+            c.wait()
+        for n in (0, 1, 8, 9):
+            first_step(some, n)
+        for n in (1, 2, 7, 8):
+            second_step(some, n)
+
+    seen = acc_ref[...] + ((observe(0) + observe(1)) + (observe(6) + observe(7)))
+    observed = (seen[0:128] + seen[128:256]) + seen[256:384]
+    obs_mean = jnp.sum(observed, axis=0, keepdims=True) * F32(1.0 / 128.0)
+    err = error_ref[...]
+    scaled = (observed - obs_mean) / (err * jnp.sqrt(F32(127.0)))
+    innovation = jnp.broadcast_to((value_ref[...] - obs_mean) / err, (8, 128))
+    turned_dot = (((1,), (1,)), ((), ()))
+    gram = lax.dot_general(scaled, scaled, turned_dot, precision=HIGHEST, preferred_element_type=F32)
+    pulled = lax.dot_general(innovation, scaled, turned_dot, precision=HIGHEST, preferred_element_type=F32)
+    deep128 = lax.broadcasted_iota(jnp.int32, (128, 128), 0)
+    diagonal = jnp.sum(jnp.where(lanes == deep128, gram, F32(0.0)), axis=0, keepdims=True)
+    rows8 = lax.broadcasted_iota(jnp.int32, (8, 128), 0)
+    extra = jnp.where(rows8 == 0, pulled, jnp.broadcast_to(diagonal, (8, 128)))
+    folded = pltpu.roll(gram[64:128], 64, 1)
+    for g in range(8):
+        cut = slice(8 * g, 8 * g + 8)
+        own, other = gram[cut], folded[cut]
+        keep = (lanes8 >= 64) | (lanes8 < rows8 + 8 * g)
+        part_ref[g, 0] = jnp.where(keep, own, other)
+        part_ref[g, 1] = extra
+
+    rs = [
+        send(part_ref.at[g], rs_ref.at[me], (rs_s, rs_r), g, dev, landed=me) for g, dev in zip(group, group_dev)
+    ]
+    for c in rs:
+        c.start()
+    rs_ref[pl.ds(me, 1)] = part_ref[pl.ds(me, 1)]
+
+    for r in range(8):
+        v = full_ref[r]
+        mean = jnp.sum(v, axis=0, keepdims=True) * F32(1.0 / 128.0)
+        mean_ref[r : r + 1, :] = mean
+        d_ref[r] = v - mean
+    store = pltpu.make_async_copy(d_ref, d_hbm, store_sem)
+    store.start()
+
+    def landed(buf, sems, sent, ids, devs, src):
+        for c in sent:
+            c.wait_send()
+        for n, dev in zip(ids, devs):
+            send(src, buf.at[n], sems, n, dev).wait_recv()
+
+    def total(buf):
+        return ((buf[0] + buf[1]) + (buf[2] + buf[3])) + ((buf[4] + buf[5]) + (buf[6] + buf[7]))
+
+    landed(rs_ref, (rs_s, rs_r), rs, group, group_dev, part_ref.at[0])
+    ysrc_ref[...] = total(rs_ref)
+    sent = [send(ysrc_ref, yin_ref.at[y], (y_s, y_r), n, dev, landed=y) for n, dev in zip(ys, y_dev)]
+    for c in sent:
+        c.start()
+    yin_ref[pl.ds(y, 1)] = ysrc_ref[...][None]
+    landed(yin_ref, (y_s, y_r), sent, ys, y_dev, ysrc_ref)
+    zsrc_ref[...] = total(yin_ref)
+    sent = [send(zsrc_ref, zin_ref.at[z], (z_s, z_r), n, dev, landed=z) for n, dev in zip(zs, z_dev)]
+    for c in sent:
+        c.start()
+    zin_ref[pl.ds(z, 1)] = zsrc_ref[...][None]
+    landed(zin_ref, (z_s, z_r), sent, zs, z_dev, zsrc_ref)
+    whole = total(zin_ref)
+    fin_ref[...] = whole[0]
+    sent = [send(fin_ref, gat_ref.at[me], (ag_s, ag_r), g, dev, landed=me) for g, dev in zip(group, group_dev)]
+    for c in sent:
+        c.start()
+    gat_ref[pl.ds(me, 1)] = whole[0:1]
+    total_ref[64:72, :] = whole[1]
+    landed(gat_ref, (ag_s, ag_r), sent, group, group_dev, fin_ref)
+    for g in range(8):
+        total_ref[8 * g : 8 * g + 8, :] = gat_ref[g]
+    store.wait()
+
+
+def front(prior, spread, courant, cells, value, error):
+    vmem, hbm = pl.BlockSpec(memory_space=pltpu.VMEM), pl.BlockSpec(memory_space=pl.ANY)
+    dma = pltpu.SemaphoreType.DMA
+    return pl.pallas_call(
+        front_kernel,
+        out_shape=(
+            jax.ShapeDtypeStruct((8, 128, 256), F32),
+            jax.ShapeDtypeStruct((8, 256), F32),
+            jax.ShapeDtypeStruct((72, 128), F32),
+        ),
+        in_specs=[hbm, vmem, vmem, vmem, vmem, vmem],
+        out_specs=(hbm, vmem, vmem),
+        scratch_shapes=[
+            pltpu.VMEM((2, 1024, 128), F32),
+            pltpu.VMEM((3, 12, 128, 128), F32),
+            pltpu.VMEM((3, 10, 128, 128), F32),
+            pltpu.VMEM((8, 128, 256), F32),
+            pltpu.VMEM((8, 128, 256), F32),
+            pltpu.VMEM((8, 256, 128), BF16),
+            pltpu.VMEM((3, 3, 16, 128), F32),
+            pltpu.VMEM((5, 3, 16, 128), F32),
+            pltpu.VMEM((2, 24, 128), F32),
+            pltpu.VMEM((2, 24, 128), F32),
+            pltpu.VMEM((2, 8, 128), F32),
+            pltpu.VMEM((2, 2, 8, 128), F32),
+            pltpu.VMEM((2, 2, 8, 128), F32),
+            pltpu.VMEM((128, 128), F32),
+            pltpu.VMEM((384, 128), F32),
+            pltpu.VMEM((8, 2, 8, 128), F32),
+            pltpu.VMEM((8, 2, 8, 128), F32),
+            pltpu.VMEM((2, 8, 128), F32),
+            pltpu.VMEM((8, 2, 8, 128), F32),
+            pltpu.VMEM((2, 8, 128), F32),
+            pltpu.VMEM((8, 2, 8, 128), F32),
+            pltpu.VMEM((8, 128), F32),
+            pltpu.VMEM((8, 8, 128), F32),
+            dma((2,)),
+            dma,
+            dma((4 * CHUNKS,)),
+            dma((4 * CHUNKS,)),
+            dma((6,)),
+            dma((6,)),
+            dma((8,)),
+            dma((8,)),
+            dma((8,)),
+            dma((8,)),
+            dma((8,)),
+            dma((8,)),
+            dma((8,)),
+            dma((8,)),
+        ],
+        compiler_params=pltpu.CompilerParams(collective_id=0, has_side_effects=True),
+        name="front",
+    )(prior, spread, courant, cells, value, error)
+
+
 def body(
     prior_sample_fields, spreading_coefficient, transport_courant, obs_cells, obs_value, obs_error
 ):
-    sample_total = prior_sample_fields.shape[0]
-    stacked = jnp.concatenate(
-        [prior_sample_fields, spreading_coefficient[None], transport_courant], axis=0
+    departures, mean, packed = front(
+        prior_sample_fields.reshape(1024, 256),
+        spreading_coefficient,
+        transport_courant.reshape(16, 256),
+        obs_cells[None, :],
+        obs_value[None, :],
+        obs_error[None, :],
     )
-    widened = with_halo(stacked, ((ROW, 1), (COL, 2)), 2)
-    members = widened[:sample_total]
-    coeffs = widened[sample_total:, 1:-1, 1:-1]
-    inner_field_block = propagate_dynamics(members, coeffs[0], coeffs[1:])
-    predicted_fields = propagate_dynamics(
-        inner_field_block, spreading_coefficient, transport_courant
-    )
-    raveled_field_vector = predicted_fields.reshape(sample_total, -1)
-    cell_total = raveled_field_vector.shape[1]
-    selector = (jnp.arange(cell_total, dtype=jnp.int32)[:, None] == obs_cells[None, :]).astype(
-        jnp.float32
-    )
-    measurement_vector = jnp.dot(raveled_field_vector, selector, precision=lax.Precision.HIGHEST)
-    sample_centroid = jnp.mean(predicted_fields, axis=0)
-    sample_departures = raveled_field_vector - sample_centroid.reshape(1, -1)
-    obs_mean = jnp.mean(measurement_vector, axis=0)
-    root = jnp.sqrt(jnp.float32(sample_total - 1))
-    scaled = (measurement_vector - obs_mean) / (obs_error * root)
-    innovation = (obs_value - obs_mean) / obs_error
-    pull_part = jnp.dot(scaled, innovation[:, None], precision=lax.Precision.HIGHEST)
-    gram_part = jnp.dot(scaled, scaled.T, precision=lax.Precision.HIGHEST)
-    gram_total, pulled = together((gram_part, pull_part), ("row_0", ("row_1", "col_0", "col_1")))
-    g = jnp.concatenate([gram_total, jnp.pad(pulled.T, ((0, 7), (0, 0)))], axis=0)
-    departures = jnp.swapaxes(sample_departures.reshape(128, 8, 256), 0, 1)
-    return tail(g, departures, sample_centroid).reshape(128, 8, 256)
+    return tail(packed, departures, mean).reshape(128, 8, 256)
 
 
 def solution(mesh):

time: 116 us -> 54.9 us (0.47)
  Pallas kernels: 7.89 us -> 54.6 us
  blocking collectives: 38 us -> 0 us
  starting transfers between devices: 25.1 us -> 0 us
  waiting for transfers between devices: 24.4 us -> 0 us
  other arithmetic: 10.3 us -> 0 us
  local copies, waits for them, and re-layouts: 7.68 us -> 0 us
  matrix products: 1.47 us -> 0 us
    pallas_call x0 -> x1, Pallas kernels: none -> 46.7 us  [front(): pl.pallas_call(front_kernel, out_shape=(jax.ShapeDtypeStruct((8, 128, 256...]
    all_to_all x2 -> x0, blocking collectives: 38 us -> none  [the longest x1 24.6 us: sent_and_summed(): parts = lax.all_to_all(cut_along(x, dim, devices), axis, 0, 0, tiled=True)]
    all_to_all x2 -> x0, waiting for transfers between devices: 15.6 us -> none  [from_everyone(): return lax.all_to_all(copies, axis, split_axis=0, concat_axis=0, tiled=True)]
    ppermute x4 -> x0, starting transfers between devices: 14.7 us -> none  [the longest x2 11.5 us: with_halo(): before = lax.ppermute(last, axis, up)]
    all_to_all x2 -> x0, starting transfers between devices: 10.3 us -> none  [from_everyone(): return lax.all_to_all(copies, axis, split_axis=0, concat_axis=0, tiled=True)]
    ppermute x4 -> x0, waiting for transfers between devices: 8.83 us -> none  [the longest x2 6.68 us: with_halo(): after = lax.ppermute(first, axis, down)]
    sub x1 -> x0, other arithmetic: 3.88 us -> none  [propagate_dynamics(): centre + spreading_coefficient * spread]
    unnamed x20 -> x0, local copies, waits for them, and re-layouts: 3.37 us -> none
  transfers between devices with their start and end apart: 6 -> 0, of which waited for: 5 -> 0; matrix products, arithmetic and copies ran while one was open for 2% -> 0% of each run, Pallas kernels for 0% -> 0%
where the time goes in v2:
time: 54.9 us; the launch traced here: 54.6 us
  Pallas kernels  54.6 us (99%)
    pallas_call x1, Pallas kernels, front(): pl.pallas_call(front_kernel, out_shape=(jax.ShapeDtypeStruct((8, 128, 256...  46.7 us
    pallas_call x1, Pallas kernels, tail(): pl.pallas_call(tail_kernel, out_shape=jax.ShapeDtypeStruct((1024, 256), F...  7.9 us

profile of v2, /device:TPU:1, one launch (start us, length us, event | category | flops | bytes accessed | tf_op | source)
XLA Modules:
  0.0 54.6 jit_solution(12623199630029053846)
XLA Ops:
  0.0 46.7 %front.1 = (f32[8,128,256]{2,1,0:T(8,128)}, f32[8,256]{1,0:T(8,128)}, f32[72,128]{1,0:T(8,128)}) custom-call(f32[1024,256]{1,0:T(8,128)} %bitcast.6, f32[8,256]{1,0:T(8,128)} %spread_ref.1, f32[16,256]{1,0:T(8,128)} %bitcast.7, s32[1,128]{1,0:T(1,128)} %bitcast.8, f32[1,128]{1,0:T(1,128)} %bitcast.9, f32[1,128]{1,0:T(1,128)} %bitcast.10), custom_call_target="tpu_custom_call" | custom-call | tf_op jit(solution)/shard_map/front/pallas_call | solution.py:470
  46.7 7.9 %tail.1 = f32[1024,256]{1,0:T(8,128)} custom-call(f32[72,128]{1,0:T(8,128)} %get-tuple-element.8.g_ref, f32[8,128,256]{2,1,0:T(8,128)} %get-tuple-element.9.d_hbm, f32[8,256]{1,0:T(8,128)} %get-tuple-element.10.mean_ref), custom_call_target="tpu_custom_call" | custom-call | tf_op jit(solution)/shard_map/tail/pallas_call | solution.py:152

commit v3 on v2

--- a/solution.py
+++ b/solution.py
@@ -95,9 +95,7 @@
             x_ref[t] = q - ((s0 + s1) + (s2 + s3))
 
 
-def tail_kernel(g_ref, d_hbm, mean_ref, out_hbm, x_ref, d_ref, dd_ref, o_ref, in_sem, out_sem):
-    fetch = pltpu.make_async_copy(d_hbm, dd_ref, in_sem)
-    fetch.start()
+def tail_kernel(g_ref, dd_ref, mean_ref, out_hbm, x_ref, d_ref, o_ref, out_sem):
     lanes = lax.broadcasted_iota(jnp.int32, (8, 128), 1)
     rows = lax.broadcasted_iota(jnp.int32, (8, 128), 0)
     upper = g_ref[0:64, :]
@@ -131,7 +129,6 @@
     w = jnp.concatenate(w, axis=0)
     whi, wlo = split2(w)
     both = jnp.concatenate([whi, wlo], axis=1)
-    fetch.wait()
     for r in range(8):
         hi, lo = split2(dd_ref[r])
         acc = jnp.dot(both, jnp.concatenate([hi, hi], axis=0), preferred_element_type=F32)
@@ -154,18 +151,17 @@
         out_shape=jax.ShapeDtypeStruct((1024, 256), F32),
         in_specs=[
             pl.BlockSpec(memory_space=pltpu.VMEM),
-            pl.BlockSpec(memory_space=pl.ANY),
+            pl.BlockSpec(memory_space=pltpu.VMEM),
             pl.BlockSpec(memory_space=pltpu.VMEM),
         ],
         out_specs=pl.BlockSpec(memory_space=pl.ANY),
         scratch_shapes=[
             pltpu.VMEM((16, 8, 128), F32),
             pltpu.VMEM((16, 8, 128), F32),
-            pltpu.VMEM((8, 128, 256), F32),
             pltpu.VMEM((2, 1024, 128), F32),
-            pltpu.SemaphoreType.DMA,
             pltpu.SemaphoreType.DMA((2,)),
         ],
+        compiler_params=pltpu.CompilerParams(vmem_limit_bytes=16 << 20),
         name="tail",
     )(g, departures, mean)
 
@@ -204,12 +200,14 @@
 
 
 def front_kernel(
-    prior_hbm, spread_ref, courant_ref, cells_ref, value_ref, error_ref,
-    d_hbm, mean_ref, total_ref,
-    nat_ref, u_ref, f_ref, full_ref, d_ref, pick_ref, raw_ref, coef_ref,
+    prior_hbm, spread_hbm, courant_hbm, cells_hbm, value_hbm, error_hbm,
+    d_ref, mean_ref, total_ref,
+    spread_ref, courant_ref, cells_ref, value_ref, error_ref,
+    nat_ref, u_ref, f_ref, full_ref, pick_ref, raw_ref, coef_ref,
     edge_ref, colin_ref, rowc_ref, rowin_ref, cor_ref, comb_ref, acc_ref,
     part_ref, rs_ref, ysrc_ref, yin_ref, zsrc_ref, zin_ref, fin_ref, gat_ref,
-    load_sem, store_sem, halo_s, halo_r, small_s, small_r, rs_s, rs_r, y_s, y_r, z_s, z_r, ag_s, ag_r,
+    more_ref, rsm_ref, ymsrc_ref, ym_ref, zmsrc_ref, zm_ref,
+    load_sem, tiny_sem, halo_s, halo_r, small_s, small_r, rs_sem, y_sem, z_sem, ag_sem,
 ):
     y, x = lax.axis_index("row_0"), lax.axis_index("row_1")
     z, core = lax.axis_index("col_0"), lax.axis_index("col_1")
@@ -225,10 +223,11 @@
 
     up, down, left, right = at_row(row - 1), at_row(row + 1), at_col(col - 1), at_col(col + 1)
     me = x * 2 + core
-    group = [lax.rem(me + i, 8) for i in range(1, 8)]
+    far_first = (4, 3, 5, 2, 6, 1, 7)
+    group = [lax.rem(me + i, 8) for i in far_first]
     group_dev = [(y, g // 2, z, lax.rem(g, 2)) for g in group]
-    ys = [lax.rem(y + i, 8) for i in range(1, 8)]
-    zs = [lax.rem(z + i, 8) for i in range(1, 8)]
+    ys = [lax.rem(y + i, 8) for i in far_first]
+    zs = [lax.rem(z + i, 8) for i in far_first]
     y_dev = [(n, x, z, core) for n in ys]
     z_dev = [(y, x, n, core) for n in zs]
 
@@ -237,11 +236,58 @@
     for device in everyone:
         pl.semaphore_signal(barrier, inc=1, device_id=device, device_id_type=MESH_IDS)
 
+    tiny = [
+        pltpu.make_async_copy(src, dst, tiny_sem.at[n])
+        for n, (src, dst) in enumerate(
+            (
+                (spread_hbm, spread_ref),
+                (courant_hbm, courant_ref),
+                (cells_hbm, cells_ref),
+                (value_hbm, value_ref),
+                (error_hbm, error_ref),
+            )
+        )
+    ]
     loads = [
-        pltpu.make_async_copy(prior_hbm.at[:, pl.ds(128 * t, 128)], nat_ref.at[t], load_sem.at[t]) for t in range(2)
+        pltpu.make_async_copy(
+            prior_hbm.at[pl.ds(part * PART * 8, PART * 8), pl.ds(128 * t, 128)],
+            nat_ref.at[t, pl.ds(part * PART * 8, PART * 8), :],
+            load_sem.at[2 * part + t],
+        )
+        for part in range(CHUNKS)
+        for t in range(2)
     ]
-    for c in loads:
+    for c in loads[:2] + tiny[:2] + loads[2:] + tiny[2:]:
         c.start()
+
+    halo = []
+    for part in range(CHUNKS):
+        some = pl.ds(part * PART, PART)
+        for t in range(2):
+            slot = part * 4 + t * 2
+            halo.append(send(u_ref.at[t, 2:4, some, :], u_ref.at[t, 10:12, some, :], (halo_s, halo_r), slot, up))
+            halo.append(send(u_ref.at[t, 8:10, some, :], u_ref.at[t, 0:2, some, :], (halo_s, halo_r), slot + 1, down))
+
+    def spread_rows(part, which):
+        for t in range(2):
+            for r in which:
+                u_ref[t, 2 + r, part * PART : part * PART + PART, :] = nat_ref[
+                    t, pl.ds(part * PART * 8 + r, PART, stride=8), :
+                ]
+
+    small = (small_s, small_r)
+    for part in range(CHUNKS):
+        for c in loads[2 * part : 2 * part + 2]:
+            c.wait()
+        spread_rows(part, (0, 1, 6, 7))
+        if part == 0:
+            pl.semaphore_wait(barrier, len(everyone))
+        for c in halo[4 * part : 4 * part + 4]:
+            c.start()
+    for part in range(CHUNKS):
+        spread_rows(part, (2, 3, 4, 5))
+    for c in tiny:
+        c.wait()
 
     lanes8 = lax.broadcasted_iota(jnp.int32, (8, 128), 1)
     for t in range(2):
@@ -259,26 +305,8 @@
         edge = jnp.where(lanes8 == n + 3, pltpu.roll(first, 3 + n, 1), edge)
     edge_ref[0, 16:24, :] = edge
     edge_ref[1, 16:24, :] = edge
-
-    for c in loads:
-        c.wait()
-    for r in (0, 1, 6, 7, 2, 3, 4, 5):
-        for t in range(2):
-            u_ref[t, 2 + r] = nat_ref[t, pl.ds(r, 128, stride=8), :]
-    pl.semaphore_wait(barrier, len(everyone))
-
-    halo = []
-    for part in range(CHUNKS):
-        some = pl.ds(part * PART, PART)
-        for t in range(2):
-            slot = part * 4 + t * 2
-            halo.append(send(u_ref.at[t, 2:4, some, :], u_ref.at[t, 10:12, some, :], (halo_s, halo_r), slot, up))
-            halo.append(send(u_ref.at[t, 8:10, some, :], u_ref.at[t, 0:2, some, :], (halo_s, halo_r), slot + 1, down))
-    small = (small_s, small_r)
     rows_out = [send(rowc_ref, rowin_ref.at[1], small, 0, up), send(rowc_ref, rowin_ref.at[0], small, 1, down)]
     for c in rows_out:
-        c.start()
-    for c in halo[:4]:
         c.start()
 
     lanes = lax.broadcasted_iota(jnp.int32, (128, 128), 1)
@@ -295,8 +323,6 @@
     ]
     for c in cols_out:
         c.start()
-    for c in halo[4:]:
-        c.start()
 
     cells = cells_ref[...]
     places = lax.broadcasted_iota(jnp.int32, (256, 128), 0)
@@ -304,7 +330,7 @@
         pick_ref[r] = jnp.where(places + 256 * r == cells, F32(1.0), F32(0.0)).astype(BF16)
 
     for c in cols_out:
-        c.wait()
+        c.wait_recv()
     corners_out = [
         send(colin_ref.at[:, 8:16, :], cor_ref.at[0], small, 4, down),
         send(colin_ref.at[:, 0:8, :], cor_ref.at[1], small, 5, up),
@@ -312,7 +338,7 @@
     for c in corners_out:
         c.start()
     for c in rows_out:
-        c.wait()
+        c.wait_recv()
 
     for n in range(3):
         for t in range(2):
@@ -347,7 +373,7 @@
         comb_ref[4 * r + 4 : 4 * r + 6, :] = colin_ref[0, 2 * r : 2 * r + 2, :]
         comb_ref[4 * r + 6 : 4 * r + 8, :] = colin_ref[1, 2 * r : 2 * r + 2, :]
     for c in corners_out:
-        c.wait()
+        c.wait_recv()
     for side in range(2):
         comb_ref[2 * side : 2 * side + 2, :] = cor_ref[0, side, 6:8, :]
         comb_ref[36 + 2 * side : 38 + 2 * side, :] = cor_ref[1, side, 0:2, :]
@@ -387,7 +413,7 @@
     for part in range(CHUNKS):
         some = slice(part * PART, part * PART + PART)
         for c in halo[4 * part : 4 * part + 4]:
-            c.wait()
+            c.wait_recv()
         for n in (0, 1, 8, 9):
             first_step(some, n)
         for n in (1, 2, 7, 8):
@@ -405,63 +431,73 @@
     deep128 = lax.broadcasted_iota(jnp.int32, (128, 128), 0)
     diagonal = jnp.sum(jnp.where(lanes == deep128, gram, F32(0.0)), axis=0, keepdims=True)
     rows8 = lax.broadcasted_iota(jnp.int32, (8, 128), 0)
-    extra = jnp.where(rows8 == 0, pulled, jnp.broadcast_to(diagonal, (8, 128)))
     folded = pltpu.roll(gram[64:128], 64, 1)
     for g in range(8):
         cut = slice(8 * g, 8 * g + 8)
-        own, other = gram[cut], folded[cut]
         keep = (lanes8 >= 64) | (lanes8 < rows8 + 8 * g)
-        part_ref[g, 0] = jnp.where(keep, own, other)
-        part_ref[g, 1] = extra
-
-    rs = [
-        send(part_ref.at[g], rs_ref.at[me], (rs_s, rs_r), g, dev, landed=me) for g, dev in zip(group, group_dev)
-    ]
-    for c in rs:
-        c.start()
+        part_ref[g] = jnp.where(keep, gram[cut], folded[cut])
+    more_ref[0:1, :] = pulled[0:1]
+    more_ref[1:2, :] = diagonal
+
+    def exchange(main, more, into, more_into, sems, place, ids, devs):
+        out = [
+            send(main(n), into.at[place], (sems[0], sems[1]), n, dev, landed=place) for n, dev in zip(ids, devs)
+        ]
+        for c in out:
+            c.start()
+        if more is not None:
+            out += [
+                send(more, more_into.at[place], (sems[2], sems[3]), n, dev, landed=place) for n, dev in zip(ids, devs)
+            ]
+            for c in out[len(ids) :]:
+                c.start()
+        return out
+
+    def landed(main, more, into, more_into, sems, ids, devs):
+        for n, dev in zip(ids, devs):
+            send(main, into.at[n], (sems[0], sems[1]), n, dev).wait_recv()
+            if more is not None:
+                send(more, more_into.at[n], (sems[2], sems[3]), n, dev).wait_recv()
+
+    def total(buf):
+        return ((buf[0] + buf[1]) + (buf[2] + buf[3])) + ((buf[4] + buf[5]) + (buf[6] + buf[7]))
+
+    rs_sems, y_sems, z_sems, ag_sems = (
+        [sems.at[n] for n in range(4)] for sems in (rs_sem, y_sem, z_sem, ag_sem)
+    )
+    rs = exchange(lambda n: part_ref.at[n], more_ref, rs_ref, rsm_ref, rs_sems, me, group, group_dev)
     rs_ref[pl.ds(me, 1)] = part_ref[pl.ds(me, 1)]
+    rsm_ref[pl.ds(me, 1)] = more_ref[...][None]
 
     for r in range(8):
         v = full_ref[r]
         mean = jnp.sum(v, axis=0, keepdims=True) * F32(1.0 / 128.0)
         mean_ref[r : r + 1, :] = mean
         d_ref[r] = v - mean
-    store = pltpu.make_async_copy(d_ref, d_hbm, store_sem)
-    store.start()
-
-    def landed(buf, sems, sent, ids, devs, src):
-        for c in sent:
-            c.wait_send()
-        for n, dev in zip(ids, devs):
-            send(src, buf.at[n], sems, n, dev).wait_recv()
-
-    def total(buf):
-        return ((buf[0] + buf[1]) + (buf[2] + buf[3])) + ((buf[4] + buf[5]) + (buf[6] + buf[7]))
-
-    landed(rs_ref, (rs_s, rs_r), rs, group, group_dev, part_ref.at[0])
+
+    landed(part_ref.at[0], more_ref, rs_ref, rsm_ref, rs_sems, group, group_dev)
     ysrc_ref[...] = total(rs_ref)
-    sent = [send(ysrc_ref, yin_ref.at[y], (y_s, y_r), n, dev, landed=y) for n, dev in zip(ys, y_dev)]
-    for c in sent:
-        c.start()
+    ymsrc_ref[...] = total(rsm_ref)
+    by_y = exchange(lambda n: ysrc_ref, ymsrc_ref, yin_ref, ym_ref, y_sems, y, ys, y_dev)
     yin_ref[pl.ds(y, 1)] = ysrc_ref[...][None]
-    landed(yin_ref, (y_s, y_r), sent, ys, y_dev, ysrc_ref)
+    ym_ref[pl.ds(y, 1)] = ymsrc_ref[...][None]
+    landed(ysrc_ref, ymsrc_ref, yin_ref, ym_ref, y_sems, ys, y_dev)
     zsrc_ref[...] = total(yin_ref)
-    sent = [send(zsrc_ref, zin_ref.at[z], (z_s, z_r), n, dev, landed=z) for n, dev in zip(zs, z_dev)]
-    for c in sent:
-        c.start()
+    zmsrc_ref[...] = total(ym_ref)
+    by_z = exchange(lambda n: zsrc_ref, zmsrc_ref, zin_ref, zm_ref, z_sems, z, zs, z_dev)
     zin_ref[pl.ds(z, 1)] = zsrc_ref[...][None]
-    landed(zin_ref, (z_s, z_r), sent, zs, z_dev, zsrc_ref)
-    whole = total(zin_ref)
-    fin_ref[...] = whole[0]
-    sent = [send(fin_ref, gat_ref.at[me], (ag_s, ag_r), g, dev, landed=me) for g, dev in zip(group, group_dev)]
-    for c in sent:
-        c.start()
-    gat_ref[pl.ds(me, 1)] = whole[0:1]
-    total_ref[64:72, :] = whole[1]
-    landed(gat_ref, (ag_s, ag_r), sent, group, group_dev, fin_ref)
+    zm_ref[pl.ds(z, 1)] = zmsrc_ref[...][None]
+    landed(zsrc_ref, zmsrc_ref, zin_ref, zm_ref, z_sems, zs, z_dev)
+    fin_ref[...] = total(zin_ref)
+    ag = exchange(lambda n: fin_ref, None, gat_ref, None, ag_sems, me, group, group_dev)
+    gat_ref[pl.ds(me, 1)] = fin_ref[...][None]
+    total_ref[64:66, :] = total(zm_ref)
+    total_ref[66:72, :] = jnp.zeros((6, 128), F32)
+    landed(fin_ref, None, gat_ref, None, ag_sems, group, group_dev)
     for g in range(8):
         total_ref[8 * g : 8 * g + 8, :] = gat_ref[g]
-    store.wait()
+    for c in halo + rows_out + cols_out + corners_out + rs + by_y + by_z + ag:
+        c.wait_send()
 
 
 def front(prior, spread, courant, cells, value, error):
@@ -470,17 +506,21 @@
     return pl.pallas_call(
         front_kernel,
         out_shape=(
-            jax.ShapeDtypeStruct((8, 128, 256), F32),
-            jax.ShapeDtypeStruct((8, 256), F32),
-            jax.ShapeDtypeStruct((72, 128), F32),
+            pltpu.VMEM((8, 128, 256), F32),
+            pltpu.VMEM((8, 256), F32),
+            pltpu.VMEM((72, 128), F32),
         ),
-        in_specs=[hbm, vmem, vmem, vmem, vmem, vmem],
-        out_specs=(hbm, vmem, vmem),
+        in_specs=[hbm] * 6,
+        out_specs=(vmem, vmem, vmem),
         scratch_shapes=[
+            pltpu.VMEM((8, 256), F32),
+            pltpu.VMEM((16, 256), F32),
+            pltpu.VMEM((1, 128), jnp.int32),
+            pltpu.VMEM((1, 128), F32),
+            pltpu.VMEM((1, 128), F32),
             pltpu.VMEM((2, 1024, 128), F32),
             pltpu.VMEM((3, 12, 128, 128), F32),
             pltpu.VMEM((3, 10, 128, 128), F32),
-            pltpu.VMEM((8, 128, 256), F32),
             pltpu.VMEM((8, 128, 256), F32),
             pltpu.VMEM((8, 256, 128), BF16),
             pltpu.VMEM((3, 3, 16, 128), F32),
@@ -492,28 +532,30 @@
             pltpu.VMEM((2, 2, 8, 128), F32),
             pltpu.VMEM((128, 128), F32),
             pltpu.VMEM((384, 128), F32),
-            pltpu.VMEM((8, 2, 8, 128), F32),
-            pltpu.VMEM((8, 2, 8, 128), F32),
-            pltpu.VMEM((2, 8, 128), F32),
-            pltpu.VMEM((8, 2, 8, 128), F32),
-            pltpu.VMEM((2, 8, 128), F32),
-            pltpu.VMEM((8, 2, 8, 128), F32),
+            pltpu.VMEM((8, 8, 128), F32),
+            pltpu.VMEM((8, 8, 128), F32),
             pltpu.VMEM((8, 128), F32),
             pltpu.VMEM((8, 8, 128), F32),
-            dma((2,)),
-            dma,
+            pltpu.VMEM((8, 128), F32),
+            pltpu.VMEM((8, 8, 128), F32),
+            pltpu.VMEM((8, 128), F32),
+            pltpu.VMEM((8, 8, 128), F32),
+            pltpu.VMEM((2, 128), F32),
+            pltpu.VMEM((8, 2, 128), F32),
+            pltpu.VMEM((2, 128), F32),
+            pltpu.VMEM((8, 2, 128), F32),
+            pltpu.VMEM((2, 128), F32),
+            pltpu.VMEM((8, 2, 128), F32),
+            dma((2 * CHUNKS,)),
+            dma((5,)),
             dma((4 * CHUNKS,)),
             dma((4 * CHUNKS,)),
             dma((6,)),
             dma((6,)),
-            dma((8,)),
-            dma((8,)),
-            dma((8,)),
-            dma((8,)),
-            dma((8,)),
-            dma((8,)),
-            dma((8,)),
-            dma((8,)),
+            dma((4, 8)),
+            dma((4, 8)),
+            dma((4, 8)),
+            dma((4, 8)),
         ],
         compiler_params=pltpu.CompilerParams(collective_id=0, has_side_effects=True),
         name="front",

time: 54.9 us -> 52 us (0.947)
  Pallas kernels: 54.6 us -> 51.8 us
    pallas_call x1, Pallas kernels: 7.9 us -> 6 us  [tail(): pl.pallas_call(tail_kernel, out_shape=jax.ShapeDtypeStruct((1024, 256), F...]
    pallas_call x1, Pallas kernels: 46.7 us -> 45.8 us  [front(): pl.pallas_call(front_kernel, out_shape=(pltpu.VMEM((8, 128, 256), F32), p...]
where the time goes in v3:
time: 52 us; the launch traced here: 51.8 us
  Pallas kernels  51.8 us (100%)
    pallas_call x1, Pallas kernels, front(): pl.pallas_call(front_kernel, out_shape=(pltpu.VMEM((8, 128, 256), F32), p...  45.8 us
    pallas_call x1, Pallas kernels, tail(): pl.pallas_call(tail_kernel, out_shape=jax.ShapeDtypeStruct((1024, 256), F...  6 us

profile of v3, /device:TPU:1, one launch (start us, length us, event | category | flops | bytes accessed | tf_op | source)
XLA Modules:
  0.0 51.8 jit_solution(16509066279811915337)
XLA Ops:
  0.0 45.8 %front.1 = (f32[8,128,256]{2,1,0:T(8,128)S(1)}, f32[8,256]{1,0:T(8,128)S(1)}, f32[72,128]{1,0:T(8,128)S(1)}) custom-call(f32[1024,256]{1,0:T(8,128)} %bitcast.6, f32[8,256]{1,0:T(8,128)} %spread_hbm.1, f32[16,256]{1,0:T(8,128)} %bitcast.7, s32[1,128]{1,0:T(1,128)} %bitcast.8, f32[1,128]{1,0:T(1,128)} %bitcast.9, f32[1,128]{1,0:T(1,128)} %bitcast.10), custom_call_target="tpu_custom_call" | custom-call | tf_op jit(solution)/shard_map/front/pallas_call | solution.py:506
  45.8 6.0 %tail.1 = f32[1024,256]{1,0:T(8,128)} custom-call(f32[72,128]{1,0:T(8,128)S(1)} %get-tuple-element.8.g_ref, f32[8,128,256]{2,1,0:T(8,128)S(1)} %get-tuple-element.9.dd_ref, f32[8,256]{1,0:T(8,128)S(1)} %get-tuple-element.10.mean_ref), custom_call_target="tpu_custom_call" | custom-call | tf_op jit(solution)/shard_map/tail/pallas_call | solution.py:149

commit v4 on v3

--- a/solution.py
+++ b/solution.py
@@ -204,7 +204,7 @@
     d_ref, mean_ref, total_ref,
     spread_ref, courant_ref, cells_ref, value_ref, error_ref,
     nat_ref, u_ref, f_ref, full_ref, pick_ref, raw_ref, coef_ref,
-    edge_ref, colin_ref, rowc_ref, rowin_ref, cor_ref, comb_ref, acc_ref,
+    edge_ref, colin_ref, rowc_ref, rowin_ref, cor_ref, comb_ref, acc_ref, give_ref, share_ref, shared_ref,
     part_ref, rs_ref, ysrc_ref, yin_ref, zsrc_ref, zin_ref, fin_ref, gat_ref,
     more_ref, rsm_ref, ymsrc_ref, ym_ref, zmsrc_ref, zm_ref,
     load_sem, tiny_sem, halo_s, halo_r, small_s, small_r, rs_sem, y_sem, z_sem, ag_sem,
@@ -261,8 +261,8 @@
         c.start()
 
     halo = []
-    for part in range(CHUNKS):
-        some = pl.ds(part * PART, PART)
+    for part in range(2):
+        some = pl.ds(part * 64, 64)
         for t in range(2):
             slot = part * 4 + t * 2
             halo.append(send(u_ref.at[t, 2:4, some, :], u_ref.at[t, 10:12, some, :], (halo_s, halo_r), slot, up))
@@ -276,16 +276,6 @@
                 ]
 
     small = (small_s, small_r)
-    for part in range(CHUNKS):
-        for c in loads[2 * part : 2 * part + 2]:
-            c.wait()
-        spread_rows(part, (0, 1, 6, 7))
-        if part == 0:
-            pl.semaphore_wait(barrier, len(everyone))
-        for c in halo[4 * part : 4 * part + 4]:
-            c.start()
-    for part in range(CHUNKS):
-        spread_rows(part, (2, 3, 4, 5))
     for c in tiny:
         c.wait()
 
@@ -296,7 +286,16 @@
             raw_ref[n, t, 1:9, :] = block
             rowc_ref[t, n : n + 1, :] = block[7:8, :]
             rowc_ref[t, n + 3 : n + 4, :] = block[0:1, :]
-        rowc_ref[t, 6:8, :] = jnp.zeros((2, 128), F32)
+            if n < 2:
+                rowc_ref[t, n + 6 : n + 7, :] = block[1:2, :]
+            if n == 0:
+                rowc_ref[t, 8:9, :] = block[6:7, :]
+        rowc_ref[t, 9:10, :] = cells_ref[...].astype(F32)
+        rowc_ref[t, 10:16, :] = jnp.zeros((6, 128), F32)
+    rows_out = [send(rowc_ref, rowin_ref.at[1], small, 0, up), send(rowc_ref, rowin_ref.at[0], small, 1, down)]
+    pl.semaphore_wait(barrier, len(everyone))
+    for c in rows_out:
+        c.start()
     edge = jnp.zeros((8, 128), F32)
     for n in range(3):
         last = spread_ref[:, 128:256] if n == 0 else courant_ref[8 * n - 8 : 8 * n, 128:256]
@@ -305,9 +304,10 @@
         edge = jnp.where(lanes8 == n + 3, pltpu.roll(first, 3 + n, 1), edge)
     edge_ref[0, 16:24, :] = edge
     edge_ref[1, 16:24, :] = edge
-    rows_out = [send(rowc_ref, rowin_ref.at[1], small, 0, up), send(rowc_ref, rowin_ref.at[0], small, 1, down)]
-    for c in rows_out:
-        c.start()
+    for part in range(CHUNKS):
+        for c in loads[2 * part : 2 * part + 2]:
+            c.wait()
+        spread_rows(part, range(8))
 
     lanes = lax.broadcasted_iota(jnp.int32, (128, 128), 1)
     ends = jnp.zeros((128, 128), F32)
@@ -329,16 +329,81 @@
     for r in range(8):
         pick_ref[r] = jnp.where(places + 256 * r == cells, F32(1.0), F32(0.0)).astype(BF16)
 
+    few = lax.broadcasted_iota(jnp.int32, (PART, 128), 1)
+    thin = lax.broadcasted_iota(jnp.int32, (1, 128), 1)
+
+    def sideways(k, t1, t):
+        w_left, w_right = k + t1, k
+        if t == 0:
+            w_left = jnp.where(thin == 0, F32(0.0), w_left)
+        else:
+            w_right = jnp.where(thin == 127, F32(0.0), w_right)
+        return w_left, w_right
+
+    def exact_parts(v):
+        hi = v.astype(BF16)
+        rest = v - hi.astype(F32)
+        mid = rest.astype(BF16)
+        lo = (rest - mid.astype(F32)).astype(BF16)
+        return jnp.concatenate([hi, mid, lo], axis=0)
+
+    for c in rows_out:
+        c.wait_recv()
+    for side in range(2):
+        a, b = ((8, 9), (3, 2))[side]
+        mine = b - 1
+        theirs, first = ((1, 3), (0, 0))[side]
+        w = []
+        for t in range(2):
+            k, t0, t1 = (raw_ref[n, t, mine : mine + 1, :] for n in range(3))
+            own = (1.0 - 4.0 * k - t0 - t1, k + t0 if side == 0 else k) + sideways(k, t1, t)
+            k, t0, t1 = (rowin_ref[theirs, t, first + n : first + n + 1, :] for n in range(3))
+            near = (1.0 - 4.0 * k - t0 - t1, k + t0 if side == 0 else k) + sideways(k, t1, t)
+            if side == 0:
+                far = rowin_ref[theirs, t, 6:7, :] + rowin_ref[theirs, t, 7:8, :]
+            else:
+                far = rowin_ref[theirs, t, 8:9, :]
+            w.append((own, near, far))
+        for part in range(CHUNKS):
+            some = slice(part * PART, part * PART + PART)
+            ub = [u_ref[t, b, some, :] for t in range(2)]
+            h = [w[t][1][1] * ub[t] for t in range(2)]
+            b_left, b_right = [pltpu.roll(v, 1, 1) for v in ub], [pltpu.roll(v, 127, 1) for v in ub]
+            h_left, h_right = [pltpu.roll(v, 1, 1) for v in h], [pltpu.roll(v, 127, 1) for v in h]
+
+            def ends_of(before, after, t):
+                if t == 0:
+                    return before[0], jnp.where(few == 127, after[1], after[0])
+                return jnp.where(few == 0, before[0], before[1]), after[1]
+
+            for t in range(2):
+                own, near, far = w[t]
+                bl, br = ends_of(b_left, b_right, t)
+                hl, hr = ends_of(h_left, h_right, t)
+                g = (own[0] * ub[t] + own[1] * u_ref[t, a, some, :]) + (own[2] * bl + own[3] * br)
+                cut = slice(128 * t, 128 * t + 128)
+                give_ref[0, some, cut] = (near[0] * h[t] + near[1] * g) + (near[2] * hl + near[3] * hr)
+                give_ref[1, some, cut] = far * h[t]
+        their_cells = rowin_ref[theirs, 0, 9:10, :]
+        spots = places.astype(F32)
+        got = jnp.zeros((384, 128), F32)
+        for n, base in enumerate(((0, 256), (1792, 1536))[side]):
+            chosen = jnp.where(spots + F32(base) == their_cells, F32(1.0), F32(0.0)).astype(BF16)
+            got = got + jnp.dot(exact_parts(give_ref[n]), chosen, preferred_element_type=F32)
+        share_ref[side] = (got[0:128] + got[128:256]) + got[256:384]
+
     for c in cols_out:
         c.wait_recv()
     corners_out = [
         send(colin_ref.at[:, 8:16, :], cor_ref.at[0], small, 4, down),
         send(colin_ref.at[:, 0:8, :], cor_ref.at[1], small, 5, up),
     ]
-    for c in corners_out:
+    shares_out = [
+        send(share_ref.at[0], shared_ref.at[0], small, 6, down),
+        send(share_ref.at[1], shared_ref.at[1], small, 7, up),
+    ]
+    for c in corners_out + shares_out + halo[:4]:
         c.start()
-    for c in rows_out:
-        c.wait_recv()
 
     for n in range(3):
         for t in range(2):
@@ -372,55 +437,63 @@
     for r in range(8):
         comb_ref[4 * r + 4 : 4 * r + 6, :] = colin_ref[0, 2 * r : 2 * r + 2, :]
         comb_ref[4 * r + 6 : 4 * r + 8, :] = colin_ref[1, 2 * r : 2 * r + 2, :]
+    turned = comb_ref[...].T
+    for n in range(1, 9):
+        u_ref[2, n + 1] = pltpu.roll(turned, (126 - 4 * n) % 128, 1)
+
+    def first_step(some, n, all_rows):
+        tiles = range(3) if 1 <= n <= 8 else range(2)
+
+        def get(t, i):
+            if not all_rows and (i in (-1, 10) or (i in (0, 9) and t < 2)):
+                return jnp.zeros((PART, 128), F32)
+            return u_ref[t, i + 1, some, :]
+
+        for t, v in zip(tiles, stencil(get, coef_ref, n, tiles, few)):
+            f_ref[t, n, some, :] = v
+
+    def second_step(some, n):
+        for t, v in zip(range(2), stencil(lambda t, i: f_ref[t, i, some, :], coef_ref, n, range(2), few)):
+            full_ref[n - 1, some, 128 * t : 128 * t + 128] = v
+
+    @pl.loop(0, CHUNKS)
+    def _(part):
+        some = pl.ds(pl.multiple_of(part * PART, PART), PART)
+        for n in range(2, 8):
+            first_step(some, n, False)
+        for n in range(3, 7):
+            second_step(some, n)
+
+    def observe(n):
+        return jnp.dot(exact_parts(full_ref[n]), pick_ref[n], preferred_element_type=F32)
+
+    acc_ref[...] = (observe(2) + observe(3)) + (observe(4) + observe(5))
+
     for c in corners_out:
         c.wait_recv()
     for side in range(2):
         comb_ref[2 * side : 2 * side + 2, :] = cor_ref[0, side, 6:8, :]
         comb_ref[36 + 2 * side : 38 + 2 * side, :] = cor_ref[1, side, 0:2, :]
     turned = comb_ref[...].T
-    for n in range(10):
+    for n in (0, 9):
         u_ref[2, n + 1] = pltpu.roll(turned, (126 - 4 * n) % 128, 1)
 
-    few = lax.broadcasted_iota(jnp.int32, (PART, 128), 1)
-
-    def first_step(some, n):
-        tiles = range(3) if 1 <= n <= 8 else range(2)
-        for t, v in zip(tiles, stencil(lambda t, i: u_ref[t, i + 1, some, :], coef_ref, n, tiles, few)):
-            f_ref[t, n, some, :] = v
-
-    def second_step(some, n):
-        for t, v in zip(range(2), stencil(lambda t, i: f_ref[t, i, some, :], coef_ref, n, range(2), few)):
-            full_ref[n - 1, some, 128 * t : 128 * t + 128] = v
+    def end_rows(some, all_rows):
+        for n in (0, 1, 8, 9):
+            first_step(some, n, all_rows)
+        for n in (1, 2, 7, 8):
+            second_step(some, n)
 
     @pl.loop(0, CHUNKS)
     def _(part):
-        some = pl.ds(pl.multiple_of(part * PART, PART), PART)
-        for n in range(2, 8):
-            first_step(some, n)
-        for n in range(3, 7):
-            second_step(some, n)
-
-    def observe(n):
-        v = full_ref[n]
-        hi = v.astype(BF16)
-        rest = v - hi.astype(F32)
-        mid = rest.astype(BF16)
-        lo = (rest - mid.astype(F32)).astype(BF16)
-        return jnp.dot(jnp.concatenate([hi, mid, lo], axis=0), pick_ref[n], preferred_element_type=F32)
-
-    acc_ref[...] = (observe(2) + observe(3)) + (observe(4) + observe(5))
-
-    for part in range(CHUNKS):
-        some = slice(part * PART, part * PART + PART)
-        for c in halo[4 * part : 4 * part + 4]:
-            c.wait_recv()
-        for n in (0, 1, 8, 9):
-            first_step(some, n)
-        for n in (1, 2, 7, 8):
-            second_step(some, n)
+        end_rows(pl.ds(pl.multiple_of(part * PART, PART), PART), False)
 
     seen = acc_ref[...] + ((observe(0) + observe(1)) + (observe(6) + observe(7)))
-    observed = (seen[0:128] + seen[128:256]) + seen[256:384]
+    for c in shares_out:
+        c.wait_recv()
+    from_up = jnp.where(row == 0, F32(0.0), F32(1.0)) * shared_ref[0]
+    from_down = jnp.where(row == 31, F32(0.0), F32(1.0)) * shared_ref[1]
+    observed = ((seen[0:128] + seen[128:256]) + seen[256:384]) + (from_up + from_down)
     obs_mean = jnp.sum(observed, axis=0, keepdims=True) * F32(1.0 / 128.0)
     err = error_ref[...]
     scaled = (observed - obs_mean) / (err * jnp.sqrt(F32(127.0)))
@@ -469,11 +542,25 @@
     rs_ref[pl.ds(me, 1)] = part_ref[pl.ds(me, 1)]
     rsm_ref[pl.ds(me, 1)] = more_ref[...][None]
 
-    for r in range(8):
-        v = full_ref[r]
-        mean = jnp.sum(v, axis=0, keepdims=True) * F32(1.0 / 128.0)
-        mean_ref[r : r + 1, :] = mean
-        d_ref[r] = v - mean
+    for c in halo[4:]:
+        c.start()
+
+    def depart(rows):
+        for r in rows:
+            v = full_ref[r]
+            mean = jnp.sum(v, axis=0, keepdims=True) * F32(1.0 / 128.0)
+            mean_ref[r : r + 1, :] = mean
+            d_ref[r] = v - mean
+
+    def finish_rows(half):
+        for c in halo[4 * half : 4 * half + 4]:
+            c.wait_recv()
+
+        @pl.loop(half * (CHUNKS // 2), (half + 1) * (CHUNKS // 2))
+        def _(part):
+            end_rows(pl.ds(pl.multiple_of(part * PART, PART), PART), True)
+
+    depart(range(2, 6))
 
     landed(part_ref.at[0], more_ref, rs_ref, rsm_ref, rs_sems, group, group_dev)
     ysrc_ref[...] = total(rs_ref)
@@ -481,12 +568,15 @@
     by_y = exchange(lambda n: ysrc_ref, ymsrc_ref, yin_ref, ym_ref, y_sems, y, ys, y_dev)
     yin_ref[pl.ds(y, 1)] = ysrc_ref[...][None]
     ym_ref[pl.ds(y, 1)] = ymsrc_ref[...][None]
+    finish_rows(0)
     landed(ysrc_ref, ymsrc_ref, yin_ref, ym_ref, y_sems, ys, y_dev)
     zsrc_ref[...] = total(yin_ref)
     zmsrc_ref[...] = total(ym_ref)
     by_z = exchange(lambda n: zsrc_ref, zmsrc_ref, zin_ref, zm_ref, z_sems, z, zs, z_dev)
     zin_ref[pl.ds(z, 1)] = zsrc_ref[...][None]
     zm_ref[pl.ds(z, 1)] = zmsrc_ref[...][None]
+    finish_rows(1)
+    depart((0, 1, 6, 7))
     landed(zsrc_ref, zmsrc_ref, zin_ref, zm_ref, z_sems, zs, z_dev)
     fin_ref[...] = total(zin_ref)
     ag = exchange(lambda n: fin_ref, None, gat_ref, None, ag_sems, me, group, group_dev)
@@ -496,7 +586,7 @@
     landed(fin_ref, None, gat_ref, None, ag_sems, group, group_dev)
     for g in range(8):
         total_ref[8 * g : 8 * g + 8, :] = gat_ref[g]
-    for c in halo + rows_out + cols_out + corners_out + rs + by_y + by_z + ag:
+    for c in halo + rows_out + cols_out + corners_out + shares_out + rs + by_y + by_z + ag:
         c.wait_send()
 
 
@@ -527,11 +617,14 @@
             pltpu.VMEM((5, 3, 16, 128), F32),
             pltpu.VMEM((2, 24, 128), F32),
             pltpu.VMEM((2, 24, 128), F32),
-            pltpu.VMEM((2, 8, 128), F32),
-            pltpu.VMEM((2, 2, 8, 128), F32),
+            pltpu.VMEM((2, 16, 128), F32),
+            pltpu.VMEM((2, 2, 16, 128), F32),
             pltpu.VMEM((2, 2, 8, 128), F32),
             pltpu.VMEM((128, 128), F32),
             pltpu.VMEM((384, 128), F32),
+            pltpu.VMEM((2, 128, 256), F32),
+            pltpu.VMEM((2, 128, 128), F32),
+            pltpu.VMEM((2, 128, 128), F32),
             pltpu.VMEM((8, 8, 128), F32),
             pltpu.VMEM((8, 8, 128), F32),
             pltpu.VMEM((8, 128), F32),
@@ -548,10 +641,10 @@
             pltpu.VMEM((8, 2, 128), F32),
             dma((2 * CHUNKS,)),
             dma((5,)),
-            dma((4 * CHUNKS,)),
-            dma((4 * CHUNKS,)),
-            dma((6,)),
-            dma((6,)),
+            dma((8,)),
+            dma((8,)),
+            dma((8,)),
+            dma((8,)),
             dma((4, 8)),
             dma((4, 8)),
             dma((4, 8)),

time: 52 us -> 50.7 us (0.975)
  Pallas kernels: 51.8 us -> 50.5 us
    pallas_call x1, Pallas kernels: 45.8 us -> 44.5 us  [front(): pl.pallas_call(front_kernel, out_shape=(pltpu.VMEM((8, 128, 256), F32), p...]
where the time goes in v4:
time: 50.7 us; the launch traced here: 50.5 us
  Pallas kernels  50.5 us (100%)
    pallas_call x1, Pallas kernels, front(): pl.pallas_call(front_kernel, out_shape=(pltpu.VMEM((8, 128, 256), F32), p...  44.5 us
    pallas_call x1, Pallas kernels, tail(): pl.pallas_call(tail_kernel, out_shape=jax.ShapeDtypeStruct((1024, 256), F...  6 us

profile of v4, /device:TPU:1, one launch (start us, length us, event | category | flops | bytes accessed | tf_op | source)
XLA Modules:
  0.0 50.5 jit_solution(10258473849849559378)
XLA Ops:
  0.0 44.5 %front.1 = (f32[8,128,256]{2,1,0:T(8,128)S(1)}, f32[8,256]{1,0:T(8,128)S(1)}, f32[72,128]{1,0:T(8,128)S(1)}) custom-call(f32[1024,256]{1,0:T(8,128)} %bitcast.6, f32[8,256]{1,0:T(8,128)} %spread_hbm.1, f32[16,256]{1,0:T(8,128)} %bitcast.7, s32[1,128]{1,0:T(1,128)} %bitcast.8, f32[1,128]{1,0:T(1,128)} %bitcast.9, f32[1,128]{1,0:T(1,128)} %bitcast.10), custom_call_target="tpu_custom_call" | custom-call | tf_op jit(solution)/shard_map/front/pallas_call | solution.py:596
  44.5 6.0 %tail.1 = f32[1024,256]{1,0:T(8,128)} custom-call(f32[72,128]{1,0:T(8,128)S(1)} %get-tuple-element.8.g_ref, f32[8,128,256]{2,1,0:T(8,128)S(1)} %get-tuple-element.9.dd_ref, f32[8,256]{1,0:T(8,128)S(1)} %get-tuple-element.10.mean_ref), custom_call_target="tpu_custom_call" | custom-call | tf_op jit(solution)/shard_map/tail/pallas_call | solution.py:149

commit v5 on v4

--- a/solution.py
+++ b/solution.py
@@ -21,6 +21,10 @@
     return jnp.broadcast_to(x[row : row + 1, :], (8, 128))
 
 
+def picked_row(x, mask):
+    return jnp.broadcast_to(jnp.sum(jnp.where(mask, x, F32(0.0)), axis=0, keepdims=True), (8, 128))
+
+
 def split2(x):
     hi = x.astype(BF16)
     lo = (x - hi.astype(F32)).astype(BF16)
@@ -34,7 +38,7 @@
         base = 8 * k
         p = x_ref[k]
         c = [lane_spread(p, base + j) for j in range(8)]
-        a = {(i, j): row_spread(c[j], i) for j in range(8) for i in range(j, 8)}
+        a = {(i, j): picked_row(c[j], rows == i) for j in range(8) for i in range(j, 8)}
         in_block = (lanes >= base) & (lanes < base + 8)
         eye = jnp.where(lanes - base == rows, F32(1.0), F32(0.0))
         p0 = jnp.where(in_block, eye, p)
@@ -168,7 +172,7 @@
 
 MESH_IDS = pl.DeviceIdType.MESH
 HIGHEST = lax.Precision.HIGHEST
-CHUNKS = 4
+CHUNKS = 2
 PART = 128 // CHUNKS
 
 
@@ -232,9 +236,37 @@
     z_dev = [(y, x, n, core) for n in zs]
 
     barrier = pltpu.get_barrier_semaphore()
-    everyone = [up, down, left, right] + group_dev + y_dev + z_dev
+    everyone = group_dev + y_dev + z_dev
+    beside = {"up": up, "down": down, "left": left, "right": right}
+    there = {"up": row > 0, "down": row < 31, "left": col > 0, "right": col < 15}
+    opposite = {"up": "down", "down": "up", "left": "right", "right": "left"}
+    for way, device in beside.items():
+
+        @pl.when(there[way])
+        def _():
+            pl.semaphore_signal(barrier, inc=1, device_id=device, device_id_type=MESH_IDS)
+
     for device in everyone:
         pl.semaphore_signal(barrier, inc=1, device_id=device, device_id_type=MESH_IDS)
+
+    def each_way(items, act, turn=lambda way: way):
+        for way in beside:
+            some = [c for c, w in items if w == way]
+            if some:
+
+                @pl.when(there[turn(way)])
+                def _():
+                    for c in some:
+                        act(c)
+
+    def begin(items):
+        each_way(items, lambda c: c.start())
+
+    def arrived(items):
+        each_way(items, lambda c: c.wait_recv(), lambda way: opposite[way])
+
+    def gone(items):
+        each_way(items, lambda c: c.wait_send())
 
     tiny = [
         pltpu.make_async_copy(src, dst, tiny_sem.at[n])
@@ -260,13 +292,31 @@
     for c in loads[:2] + tiny[:2] + loads[2:] + tiny[2:]:
         c.start()
 
+    for side, way in enumerate(("up", "down")):
+
+        @pl.when(jnp.logical_not(there[way]))
+        def _():
+            rowin_ref[side] = jnp.zeros((2, 16, 128), F32)
+            cor_ref[side] = jnp.zeros((2, 8, 128), F32)
+            shared_ref[side] = jnp.zeros((128, 128), F32)
+            for t in range(2):
+                for n in range(2):
+                    u_ref[t, 10 * side + n] = jnp.zeros((128, 128), F32)
+
+    for side, way in enumerate(("left", "right")):
+
+        @pl.when(jnp.logical_not(there[way]))
+        def _():
+            colin_ref[side] = jnp.zeros((24, 128), F32)
+
     halo = []
     for part in range(2):
         some = pl.ds(part * 64, 64)
         for t in range(2):
             slot = part * 4 + t * 2
-            halo.append(send(u_ref.at[t, 2:4, some, :], u_ref.at[t, 10:12, some, :], (halo_s, halo_r), slot, up))
-            halo.append(send(u_ref.at[t, 8:10, some, :], u_ref.at[t, 0:2, some, :], (halo_s, halo_r), slot + 1, down))
+            sems = (halo_s, halo_r)
+            halo.append((send(u_ref.at[t, 2:4, some, :], u_ref.at[t, 10:12, some, :], sems, slot, up), "up"))
+            halo.append((send(u_ref.at[t, 8:10, some, :], u_ref.at[t, 0:2, some, :], sems, slot + 1, down), "down"))
 
     def spread_rows(part, which):
         for t in range(2):
@@ -292,10 +342,13 @@
                 rowc_ref[t, 8:9, :] = block[6:7, :]
         rowc_ref[t, 9:10, :] = cells_ref[...].astype(F32)
         rowc_ref[t, 10:16, :] = jnp.zeros((6, 128), F32)
-    rows_out = [send(rowc_ref, rowin_ref.at[1], small, 0, up), send(rowc_ref, rowin_ref.at[0], small, 1, down)]
-    pl.semaphore_wait(barrier, len(everyone))
-    for c in rows_out:
-        c.start()
+    rows_out = [
+        (send(rowc_ref, rowin_ref.at[1], small, 0, up), "up"),
+        (send(rowc_ref, rowin_ref.at[0], small, 1, down), "down"),
+    ]
+    at_border = (32 - row) // 32 + (row + 1) // 32 + (16 - col) // 16 + (col + 1) // 16
+    pl.semaphore_wait(barrier, len(everyone) + 4 - at_border)
+    begin(rows_out)
     edge = jnp.zeros((8, 128), F32)
     for n in range(3):
         last = spread_ref[:, 128:256] if n == 0 else courant_ref[8 * n - 8 : 8 * n, 128:256]
@@ -318,11 +371,10 @@
     edge_ref[0, 0:16, :] = ends[0:16]
     edge_ref[1, 0:16, :] = ends[16:32]
     cols_out = [
-        send(edge_ref.at[0], colin_ref.at[0], small, 2, right),
-        send(edge_ref.at[1], colin_ref.at[1], small, 3, left),
+        (send(edge_ref.at[0], colin_ref.at[0], small, 2, right), "right"),
+        (send(edge_ref.at[1], colin_ref.at[1], small, 3, left), "left"),
     ]
-    for c in cols_out:
-        c.start()
+    begin(cols_out)
 
     cells = cells_ref[...]
     places = lax.broadcasted_iota(jnp.int32, (256, 128), 0)
@@ -347,8 +399,7 @@
         lo = (rest - mid.astype(F32)).astype(BF16)
         return jnp.concatenate([hi, mid, lo], axis=0)
 
-    for c in rows_out:
-        c.wait_recv()
+    arrived(rows_out)
     for side in range(2):
         a, b = ((8, 9), (3, 2))[side]
         mine = b - 1
@@ -392,18 +443,16 @@
             got = got + jnp.dot(exact_parts(give_ref[n]), chosen, preferred_element_type=F32)
         share_ref[side] = (got[0:128] + got[128:256]) + got[256:384]
 
-    for c in cols_out:
-        c.wait_recv()
+    arrived(cols_out)
     corners_out = [
-        send(colin_ref.at[:, 8:16, :], cor_ref.at[0], small, 4, down),
-        send(colin_ref.at[:, 0:8, :], cor_ref.at[1], small, 5, up),
+        (send(colin_ref.at[:, 8:16, :], cor_ref.at[0], small, 4, down), "down"),
+        (send(colin_ref.at[:, 0:8, :], cor_ref.at[1], small, 5, up), "up"),
     ]
     shares_out = [
-        send(share_ref.at[0], shared_ref.at[0], small, 6, down),
-        send(share_ref.at[1], shared_ref.at[1], small, 7, up),
+        (send(share_ref.at[0], shared_ref.at[0], small, 6, down), "down"),
+        (send(share_ref.at[1], shared_ref.at[1], small, 7, up), "up"),
     ]
-    for c in corners_out + shares_out + halo[:4]:
-        c.start()
+    begin(corners_out + shares_out + halo[:4])
 
     for n in range(3):
         for t in range(2):
@@ -469,8 +518,7 @@
 
     acc_ref[...] = (observe(2) + observe(3)) + (observe(4) + observe(5))
 
-    for c in corners_out:
-        c.wait_recv()
+    arrived(corners_out)
     for side in range(2):
         comb_ref[2 * side : 2 * side + 2, :] = cor_ref[0, side, 6:8, :]
         comb_ref[36 + 2 * side : 38 + 2 * side, :] = cor_ref[1, side, 0:2, :]
@@ -489,11 +537,8 @@
         end_rows(pl.ds(pl.multiple_of(part * PART, PART), PART), False)
 
     seen = acc_ref[...] + ((observe(0) + observe(1)) + (observe(6) + observe(7)))
-    for c in shares_out:
-        c.wait_recv()
-    from_up = jnp.where(row == 0, F32(0.0), F32(1.0)) * shared_ref[0]
-    from_down = jnp.where(row == 31, F32(0.0), F32(1.0)) * shared_ref[1]
-    observed = ((seen[0:128] + seen[128:256]) + seen[256:384]) + (from_up + from_down)
+    arrived(shares_out)
+    observed = ((seen[0:128] + seen[128:256]) + seen[256:384]) + (shared_ref[0] + shared_ref[1])
     obs_mean = jnp.sum(observed, axis=0, keepdims=True) * F32(1.0 / 128.0)
     err = error_ref[...]
     scaled = (observed - obs_mean) / (err * jnp.sqrt(F32(127.0)))
@@ -542,8 +587,7 @@
     rs_ref[pl.ds(me, 1)] = part_ref[pl.ds(me, 1)]
     rsm_ref[pl.ds(me, 1)] = more_ref[...][None]
 
-    for c in halo[4:]:
-        c.start()
+    begin(halo[4:])
 
     def depart(rows):
         for r in rows:
@@ -553,8 +597,7 @@
             d_ref[r] = v - mean
 
     def finish_rows(half):
-        for c in halo[4 * half : 4 * half + 4]:
-            c.wait_recv()
+        arrived(halo[4 * half : 4 * half + 4])
 
         @pl.loop(half * (CHUNKS // 2), (half + 1) * (CHUNKS // 2))
         def _(part):
@@ -586,7 +629,8 @@
     landed(fin_ref, None, gat_ref, None, ag_sems, group, group_dev)
     for g in range(8):
         total_ref[8 * g : 8 * g + 8, :] = gat_ref[g]
-    for c in halo + rows_out + cols_out + corners_out + shares_out + rs + by_y + by_z + ag:
+    gone(halo + rows_out + cols_out + corners_out + shares_out)
+    for c in rs + by_y + by_z + ag:
         c.wait_send()
 
 

time: 50.7 us -> 49.4 us (0.974)
  Pallas kernels: 50.5 us -> 49.2 us
    pallas_call x1, Pallas kernels: 6 us -> 5.01 us  [tail(): pl.pallas_call(tail_kernel, out_shape=jax.ShapeDtypeStruct((1024, 256), F...]
where the time goes in v5:
time: 49.4 us; the launch traced here: 49.2 us
  Pallas kernels  49.2 us (100%)
    pallas_call x1, Pallas kernels, front(): pl.pallas_call(front_kernel, out_shape=(pltpu.VMEM((8, 128, 256), F32), p...  44.2 us
    pallas_call x1, Pallas kernels, tail(): pl.pallas_call(tail_kernel, out_shape=jax.ShapeDtypeStruct((1024, 256), F...  5.01 us

profile of v5, /device:TPU:1, one launch (start us, length us, event | category | flops | bytes accessed | tf_op | source)
XLA Modules:
  0.0 49.2 jit_solution(8034480079409587752)
XLA Ops:
  0.0 44.2 %front.1 = (f32[8,128,256]{2,1,0:T(8,128)S(1)}, f32[8,256]{1,0:T(8,128)S(1)}, f32[72,128]{1,0:T(8,128)S(1)}) custom-call(f32[1024,256]{1,0:T(8,128)} %bitcast.6, f32[8,256]{1,0:T(8,128)} %spread_hbm.1, f32[16,256]{1,0:T(8,128)} %bitcast.7, s32[1,128]{1,0:T(1,128)} %bitcast.8, f32[1,128]{1,0:T(1,128)} %bitcast.9, f32[1,128]{1,0:T(1,128)} %bitcast.10), custom_call_target="tpu_custom_call" | custom-call | tf_op jit(solution)/shard_map/front/pallas_call | solution.py:640
  44.2 5.0 %tail.1 = f32[1024,256]{1,0:T(8,128)} custom-call(f32[72,128]{1,0:T(8,128)S(1)} %get-tuple-element.8.g_ref, f32[8,128,256]{2,1,0:T(8,128)S(1)} %get-tuple-element.9.dd_ref, f32[8,256]{1,0:T(8,128)S(1)} %get-tuple-element.10.mean_ref), custom_call_target="tpu_custom_call" | custom-call | tf_op jit(solution)/shard_map/tail/pallas_call | solution.py:153

commit v6 on v5

--- a/solution.py
+++ b/solution.py
@@ -210,7 +210,6 @@
     nat_ref, u_ref, f_ref, full_ref, pick_ref, raw_ref, coef_ref,
     edge_ref, colin_ref, rowc_ref, rowin_ref, cor_ref, comb_ref, acc_ref, give_ref, share_ref, shared_ref,
     part_ref, rs_ref, ysrc_ref, yin_ref, zsrc_ref, zin_ref, fin_ref, gat_ref,
-    more_ref, rsm_ref, ymsrc_ref, ym_ref, zmsrc_ref, zm_ref,
     load_sem, tiny_sem, halo_s, halo_r, small_s, small_r, rs_sem, y_sem, z_sem, ag_sem,
 ):
     y, x = lax.axis_index("row_0"), lax.axis_index("row_1")
@@ -224,6 +223,9 @@
     def at_col(n):
         n = lax.rem(n + 16, 16)
         return (y, x, n // 2, lax.rem(n, 2))
+
+    def at_both(m, n):
+        return at_row(m)[:2] + at_col(n)[2:]
 
     up, down, left, right = at_row(row - 1), at_row(row + 1), at_col(col - 1), at_col(col + 1)
     me = x * 2 + core
@@ -237,9 +239,22 @@
 
     barrier = pltpu.get_barrier_semaphore()
     everyone = group_dev + y_dev + z_dev
-    beside = {"up": up, "down": down, "left": left, "right": right}
+    beside = {
+        "up": up,
+        "down": down,
+        "left": left,
+        "right": right,
+        "up left": at_both(row - 1, col - 1),
+        "up right": at_both(row - 1, col + 1),
+        "down left": at_both(row + 1, col - 1),
+        "down right": at_both(row + 1, col + 1),
+    }
     there = {"up": row > 0, "down": row < 31, "left": col > 0, "right": col < 15}
     opposite = {"up": "down", "down": "up", "left": "right", "right": "left"}
+    for v in ("up", "down"):
+        for h in ("left", "right"):
+            there[f"{v} {h}"] = there[v] & there[h]
+            opposite[f"{v} {h}"] = f"{opposite[v]} {opposite[h]}"
     for way, device in beside.items():
 
         @pl.when(there[way])
@@ -297,7 +312,6 @@
         @pl.when(jnp.logical_not(there[way]))
         def _():
             rowin_ref[side] = jnp.zeros((2, 16, 128), F32)
-            cor_ref[side] = jnp.zeros((2, 8, 128), F32)
             shared_ref[side] = jnp.zeros((128, 128), F32)
             for t in range(2):
                 for n in range(2):
@@ -324,6 +338,13 @@
                 u_ref[t, 2 + r, part * PART : part * PART + PART, :] = nat_ref[
                     t, pl.ds(part * PART * 8 + r, PART, stride=8), :
                 ]
+
+    for v in range(2):
+        for h in range(2):
+
+            @pl.when(jnp.logical_not(there[("up", "down")[v] + (" left", " right")[h]]))
+            def _():
+                cor_ref[v, h] = jnp.zeros((8, 128), F32)
 
     small = (small_s, small_r)
     for c in tiny:
@@ -346,8 +367,9 @@
         (send(rowc_ref, rowin_ref.at[1], small, 0, up), "up"),
         (send(rowc_ref, rowin_ref.at[0], small, 1, down), "down"),
     ]
-    at_border = (32 - row) // 32 + (row + 1) // 32 + (16 - col) // 16 + (col + 1) // 16
-    pl.semaphore_wait(barrier, len(everyone) + 4 - at_border)
+    rows_near = 2 - (32 - row) // 32 - (row + 1) // 32
+    cols_near = 2 - (16 - col) // 16 - (col + 1) // 16
+    pl.semaphore_wait(barrier, len(everyone) + rows_near + cols_near + rows_near * cols_near)
     begin(rows_out)
     edge = jnp.zeros((8, 128), F32)
     for n in range(3):
@@ -374,7 +396,14 @@
         (send(edge_ref.at[0], colin_ref.at[0], small, 2, right), "right"),
         (send(edge_ref.at[1], colin_ref.at[1], small, 3, left), "left"),
     ]
-    begin(cols_out)
+    corners_out = [
+        (send(edge_ref.at[0, 8:16, :], cor_ref.at[0, 0], small, 4, beside["down right"]), "down right"),
+        (send(edge_ref.at[1, 8:16, :], cor_ref.at[0, 1], small, 5, beside["down left"]), "down left"),
+        (send(edge_ref.at[0, 0:8, :], cor_ref.at[1, 0], small, 8, beside["up right"]), "up right"),
+        (send(edge_ref.at[1, 0:8, :], cor_ref.at[1, 1], small, 9, beside["up left"]), "up left"),
+    ]
+    begin(cols_out + corners_out)
+    begin(halo[:4])
 
     cells = cells_ref[...]
     places = lax.broadcasted_iota(jnp.int32, (256, 128), 0)
@@ -443,16 +472,13 @@
             got = got + jnp.dot(exact_parts(give_ref[n]), chosen, preferred_element_type=F32)
         share_ref[side] = (got[0:128] + got[128:256]) + got[256:384]
 
-    arrived(cols_out)
-    corners_out = [
-        (send(colin_ref.at[:, 8:16, :], cor_ref.at[0], small, 4, down), "down"),
-        (send(colin_ref.at[:, 0:8, :], cor_ref.at[1], small, 5, up), "up"),
-    ]
     shares_out = [
         (send(share_ref.at[0], shared_ref.at[0], small, 6, down), "down"),
         (send(share_ref.at[1], shared_ref.at[1], small, 7, up), "up"),
     ]
-    begin(corners_out + shares_out + halo[:4])
+    begin(shares_out)
+    begin(halo[4:])
+    arrived(cols_out)
 
     for n in range(3):
         for t in range(2):
@@ -553,41 +579,25 @@
     for g in range(8):
         cut = slice(8 * g, 8 * g + 8)
         keep = (lanes8 >= 64) | (lanes8 < rows8 + 8 * g)
-        part_ref[g] = jnp.where(keep, gram[cut], folded[cut])
-    more_ref[0:1, :] = pulled[0:1]
-    more_ref[1:2, :] = diagonal
-
-    def exchange(main, more, into, more_into, sems, place, ids, devs):
-        out = [
-            send(main(n), into.at[place], (sems[0], sems[1]), n, dev, landed=place) for n, dev in zip(ids, devs)
-        ]
+        part_ref[g, 0:8, :] = jnp.where(keep, gram[cut], folded[cut])
+        part_ref[g, 8:9, :] = pulled[0:1]
+        part_ref[g, 9:10, :] = diagonal
+
+    def exchange(main, into, sems, place, ids, devs):
+        out = [send(main(n), into.at[place], (sems.at[0], sems.at[1]), n, dev, landed=place) for n, dev in zip(ids, devs)]
         for c in out:
             c.start()
-        if more is not None:
-            out += [
-                send(more, more_into.at[place], (sems[2], sems[3]), n, dev, landed=place) for n, dev in zip(ids, devs)
-            ]
-            for c in out[len(ids) :]:
-                c.start()
         return out
 
-    def landed(main, more, into, more_into, sems, ids, devs):
+    def landed(main, into, sems, ids, devs):
         for n, dev in zip(ids, devs):
-            send(main, into.at[n], (sems[0], sems[1]), n, dev).wait_recv()
-            if more is not None:
-                send(more, more_into.at[n], (sems[2], sems[3]), n, dev).wait_recv()
+            send(main, into.at[n], (sems.at[0], sems.at[1]), n, dev).wait_recv()
 
     def total(buf):
         return ((buf[0] + buf[1]) + (buf[2] + buf[3])) + ((buf[4] + buf[5]) + (buf[6] + buf[7]))
 
-    rs_sems, y_sems, z_sems, ag_sems = (
-        [sems.at[n] for n in range(4)] for sems in (rs_sem, y_sem, z_sem, ag_sem)
-    )
-    rs = exchange(lambda n: part_ref.at[n], more_ref, rs_ref, rsm_ref, rs_sems, me, group, group_dev)
+    rs = exchange(lambda n: part_ref.at[n], rs_ref, rs_sem, me, group, group_dev)
     rs_ref[pl.ds(me, 1)] = part_ref[pl.ds(me, 1)]
-    rsm_ref[pl.ds(me, 1)] = more_ref[...][None]
-
-    begin(halo[4:])
 
     def depart(rows):
         for r in rows:
@@ -605,28 +615,25 @@
 
     depart(range(2, 6))
 
-    landed(part_ref.at[0], more_ref, rs_ref, rsm_ref, rs_sems, group, group_dev)
+    landed(part_ref.at[0], rs_ref, rs_sem, group, group_dev)
     ysrc_ref[...] = total(rs_ref)
-    ymsrc_ref[...] = total(rsm_ref)
-    by_y = exchange(lambda n: ysrc_ref, ymsrc_ref, yin_ref, ym_ref, y_sems, y, ys, y_dev)
+    by_y = exchange(lambda n: ysrc_ref, yin_ref, y_sem, y, ys, y_dev)
     yin_ref[pl.ds(y, 1)] = ysrc_ref[...][None]
-    ym_ref[pl.ds(y, 1)] = ymsrc_ref[...][None]
     finish_rows(0)
-    landed(ysrc_ref, ymsrc_ref, yin_ref, ym_ref, y_sems, ys, y_dev)
+    landed(ysrc_ref, yin_ref, y_sem, ys, y_dev)
     zsrc_ref[...] = total(yin_ref)
-    zmsrc_ref[...] = total(ym_ref)
-    by_z = exchange(lambda n: zsrc_ref, zmsrc_ref, zin_ref, zm_ref, z_sems, z, zs, z_dev)
+    by_z = exchange(lambda n: zsrc_ref, zin_ref, z_sem, z, zs, z_dev)
     zin_ref[pl.ds(z, 1)] = zsrc_ref[...][None]
-    zm_ref[pl.ds(z, 1)] = zmsrc_ref[...][None]
     finish_rows(1)
     depart((0, 1, 6, 7))
-    landed(zsrc_ref, zmsrc_ref, zin_ref, zm_ref, z_sems, zs, z_dev)
-    fin_ref[...] = total(zin_ref)
-    ag = exchange(lambda n: fin_ref, None, gat_ref, None, ag_sems, me, group, group_dev)
+    landed(zsrc_ref, zin_ref, z_sem, zs, z_dev)
+    whole = total(zin_ref)
+    fin_ref[...] = whole[0:8]
+    ag = exchange(lambda n: fin_ref, gat_ref, ag_sem, me, group, group_dev)
     gat_ref[pl.ds(me, 1)] = fin_ref[...][None]
-    total_ref[64:66, :] = total(zm_ref)
+    total_ref[64:66, :] = whole[8:10]
     total_ref[66:72, :] = jnp.zeros((6, 128), F32)
-    landed(fin_ref, None, gat_ref, None, ag_sems, group, group_dev)
+    landed(fin_ref, gat_ref, ag_sem, group, group_dev)
     for g in range(8):
         total_ref[8 * g : 8 * g + 8, :] = gat_ref[g]
     gone(halo + rows_out + cols_out + corners_out + shares_out)
@@ -669,30 +676,24 @@
             pltpu.VMEM((2, 128, 256), F32),
             pltpu.VMEM((2, 128, 128), F32),
             pltpu.VMEM((2, 128, 128), F32),
-            pltpu.VMEM((8, 8, 128), F32),
-            pltpu.VMEM((8, 8, 128), F32),
+            pltpu.VMEM((8, 10, 128), F32),
+            pltpu.VMEM((8, 10, 128), F32),
+            pltpu.VMEM((10, 128), F32),
+            pltpu.VMEM((8, 10, 128), F32),
+            pltpu.VMEM((10, 128), F32),
+            pltpu.VMEM((8, 10, 128), F32),
             pltpu.VMEM((8, 128), F32),
             pltpu.VMEM((8, 8, 128), F32),
-            pltpu.VMEM((8, 128), F32),
-            pltpu.VMEM((8, 8, 128), F32),
-            pltpu.VMEM((8, 128), F32),
-            pltpu.VMEM((8, 8, 128), F32),
-            pltpu.VMEM((2, 128), F32),
-            pltpu.VMEM((8, 2, 128), F32),
-            pltpu.VMEM((2, 128), F32),
-            pltpu.VMEM((8, 2, 128), F32),
-            pltpu.VMEM((2, 128), F32),
-            pltpu.VMEM((8, 2, 128), F32),
             dma((2 * CHUNKS,)),
             dma((5,)),
             dma((8,)),
             dma((8,)),
-            dma((8,)),
-            dma((8,)),
-            dma((4, 8)),
-            dma((4, 8)),
-            dma((4, 8)),
-            dma((4, 8)),
+            dma((10,)),
+            dma((10,)),
+            dma((2, 8)),
+            dma((2, 8)),
+            dma((2, 8)),
+            dma((2, 8)),
         ],
         compiler_params=pltpu.CompilerParams(collective_id=0, has_side_effects=True),
         name="front",

time: 49.4 us -> 47.5 us (0.962)
  Pallas kernels: 49.2 us -> 47.4 us
    pallas_call x1, Pallas kernels: 44.2 us -> 42.4 us  [front(): pl.pallas_call(front_kernel, out_shape=(pltpu.VMEM((8, 128, 256), F32), p...]
where the time goes in v6:
time: 47.5 us; the launch traced here: 47.4 us
  Pallas kernels  47.4 us (100%)
    pallas_call x1, Pallas kernels, front(): pl.pallas_call(front_kernel, out_shape=(pltpu.VMEM((8, 128, 256), F32), p...  42.4 us
    pallas_call x1, Pallas kernels, tail(): pl.pallas_call(tail_kernel, out_shape=jax.ShapeDtypeStruct((1024, 256), F...  5.01 us

profile of v6, /device:TPU:1, one launch (start us, length us, event | category | flops | bytes accessed | tf_op | source)
XLA Modules:
  0.0 47.4 jit_solution(6774126932464775771)
XLA Ops:
  0.0 42.4 %front.1 = (f32[8,128,256]{2,1,0:T(8,128)S(1)}, f32[8,256]{1,0:T(8,128)S(1)}, f32[72,128]{1,0:T(8,128)S(1)}) custom-call(f32[1024,256]{1,0:T(8,128)} %bitcast.6, f32[8,256]{1,0:T(8,128)} %spread_hbm.1, f32[16,256]{1,0:T(8,128)} %bitcast.7, s32[1,128]{1,0:T(1,128)} %bitcast.8, f32[1,128]{1,0:T(1,128)} %bitcast.9, f32[1,128]{1,0:T(1,128)} %bitcast.10), custom_call_target="tpu_custom_call" | custom-call | tf_op jit(solution)/shard_map/front/pallas_call | solution.py:647
  42.4 5.0 %tail.1 = f32[1024,256]{1,0:T(8,128)} custom-call(f32[72,128]{1,0:T(8,128)S(1)} %get-tuple-element.8.g_ref, f32[8,128,256]{2,1,0:T(8,128)S(1)} %get-tuple-element.9.dd_ref, f32[8,256]{1,0:T(8,128)S(1)} %get-tuple-element.10.mean_ref), custom_call_target="tpu_custom_call" | custom-call | tf_op jit(solution)/shard_map/tail/pallas_call | solution.py:153

commit v7 on v6

--- a/solution.py
+++ b/solution.py
@@ -311,7 +311,7 @@
 
         @pl.when(jnp.logical_not(there[way]))
         def _():
-            rowin_ref[side] = jnp.zeros((2, 16, 128), F32)
+            rowin_ref[side] = jnp.zeros((2, 8, 128), F32)
             shared_ref[side] = jnp.zeros((128, 128), F32)
             for t in range(2):
                 for n in range(2):
@@ -355,17 +355,19 @@
         cut = slice(128 * t, 128 * t + 128)
         for n, block in enumerate((spread_ref[:, cut], courant_ref[0:8, cut], courant_ref[8:16, cut])):
             raw_ref[n, t, 1:9, :] = block
-            rowc_ref[t, n : n + 1, :] = block[7:8, :]
-            rowc_ref[t, n + 3 : n + 4, :] = block[0:1, :]
+            rowc_ref[0, t, n : n + 1, :] = block[0:1, :]
+            rowc_ref[1, t, n : n + 1, :] = block[7:8, :]
             if n < 2:
-                rowc_ref[t, n + 6 : n + 7, :] = block[1:2, :]
+                rowc_ref[0, t, n + 3 : n + 4, :] = block[1:2, :]
             if n == 0:
-                rowc_ref[t, 8:9, :] = block[6:7, :]
-        rowc_ref[t, 9:10, :] = cells_ref[...].astype(F32)
-        rowc_ref[t, 10:16, :] = jnp.zeros((6, 128), F32)
+                rowc_ref[1, t, 3:4, :] = block[6:7, :]
+        for way in range(2):
+            rowc_ref[way, t, 5:6, :] = cells_ref[...].astype(F32)
+            rowc_ref[way, t, 6:8, :] = jnp.zeros((2, 128), F32)
+        rowc_ref[1, t, 4:5, :] = jnp.zeros((1, 128), F32)
     rows_out = [
-        (send(rowc_ref, rowin_ref.at[1], small, 0, up), "up"),
-        (send(rowc_ref, rowin_ref.at[0], small, 1, down), "down"),
+        (send(rowc_ref.at[0], rowin_ref.at[1], small, 0, up), "up"),
+        (send(rowc_ref.at[1], rowin_ref.at[0], small, 1, down), "down"),
     ]
     rows_near = 2 - (32 - row) // 32 - (row + 1) // 32
     cols_near = 2 - (16 - col) // 16 - (col + 1) // 16
@@ -429,20 +431,24 @@
         return jnp.concatenate([hi, mid, lo], axis=0)
 
     arrived(rows_out)
+    shares_out = [
+        (send(share_ref.at[0], shared_ref.at[0], small, 6, down), "down"),
+        (send(share_ref.at[1], shared_ref.at[1], small, 7, up), "up"),
+    ]
     for side in range(2):
         a, b = ((8, 9), (3, 2))[side]
         mine = b - 1
-        theirs, first = ((1, 3), (0, 0))[side]
+        theirs = 1 - side
         w = []
         for t in range(2):
             k, t0, t1 = (raw_ref[n, t, mine : mine + 1, :] for n in range(3))
             own = (1.0 - 4.0 * k - t0 - t1, k + t0 if side == 0 else k) + sideways(k, t1, t)
-            k, t0, t1 = (rowin_ref[theirs, t, first + n : first + n + 1, :] for n in range(3))
+            k, t0, t1 = (rowin_ref[theirs, t, n : n + 1, :] for n in range(3))
             near = (1.0 - 4.0 * k - t0 - t1, k + t0 if side == 0 else k) + sideways(k, t1, t)
             if side == 0:
-                far = rowin_ref[theirs, t, 6:7, :] + rowin_ref[theirs, t, 7:8, :]
+                far = rowin_ref[theirs, t, 3:4, :] + rowin_ref[theirs, t, 4:5, :]
             else:
-                far = rowin_ref[theirs, t, 8:9, :]
+                far = rowin_ref[theirs, t, 3:4, :]
             w.append((own, near, far))
         for part in range(CHUNKS):
             some = slice(part * PART, part * PART + PART)
@@ -464,26 +470,22 @@
                 cut = slice(128 * t, 128 * t + 128)
                 give_ref[0, some, cut] = (near[0] * h[t] + near[1] * g) + (near[2] * hl + near[3] * hr)
                 give_ref[1, some, cut] = far * h[t]
-        their_cells = rowin_ref[theirs, 0, 9:10, :]
+        their_cells = rowin_ref[theirs, 0, 5:6, :]
         spots = places.astype(F32)
         got = jnp.zeros((384, 128), F32)
         for n, base in enumerate(((0, 256), (1792, 1536))[side]):
             chosen = jnp.where(spots + F32(base) == their_cells, F32(1.0), F32(0.0)).astype(BF16)
             got = got + jnp.dot(exact_parts(give_ref[n]), chosen, preferred_element_type=F32)
         share_ref[side] = (got[0:128] + got[128:256]) + got[256:384]
-
-    shares_out = [
-        (send(share_ref.at[0], shared_ref.at[0], small, 6, down), "down"),
-        (send(share_ref.at[1], shared_ref.at[1], small, 7, up), "up"),
-    ]
-    begin(shares_out)
+        begin(shares_out[side : side + 1])
+
     begin(halo[4:])
     arrived(cols_out)
 
     for n in range(3):
         for t in range(2):
             raw_ref[n, t, 0:1, :] = rowin_ref[0, t, n : n + 1, :]
-            raw_ref[n, t, 9:10, :] = rowin_ref[1, t, n + 3 : n + 4, :]
+            raw_ref[n, t, 9:10, :] = rowin_ref[1, t, n : n + 1, :]
         beyond = jnp.where(
             lanes8 == 127,
             pltpu.roll(colin_ref[0, 16:24, :], 127 - n, 1),
@@ -668,8 +670,8 @@
             pltpu.VMEM((5, 3, 16, 128), F32),
             pltpu.VMEM((2, 24, 128), F32),
             pltpu.VMEM((2, 24, 128), F32),
-            pltpu.VMEM((2, 16, 128), F32),
-            pltpu.VMEM((2, 2, 16, 128), F32),
+            pltpu.VMEM((2, 2, 8, 128), F32),
+            pltpu.VMEM((2, 2, 8, 128), F32),
             pltpu.VMEM((2, 2, 8, 128), F32),
             pltpu.VMEM((128, 128), F32),
             pltpu.VMEM((384, 128), F32),

time: 47.5 us -> 47.2 us (level)
  no operation moved by 1% of the time
where the time goes in v7:
time: 47.2 us; the launch traced here: 47.1 us
  Pallas kernels  47.1 us (100%)
    pallas_call x1, Pallas kernels, front(): pl.pallas_call(front_kernel, out_shape=(pltpu.VMEM((8, 128, 256), F32), p...  42.1 us
    pallas_call x1, Pallas kernels, tail(): pl.pallas_call(tail_kernel, out_shape=jax.ShapeDtypeStruct((1024, 256), F...  5.01 us

profile of v7, /device:TPU:1, one launch (start us, length us, event | category | flops | bytes accessed | tf_op | source)
XLA Modules:
  0.0 47.1 jit_solution(4732274998322425857)
XLA Ops:
  0.0 42.1 %front.1 = (f32[8,128,256]{2,1,0:T(8,128)S(1)}, f32[8,256]{1,0:T(8,128)S(1)}, f32[72,128]{1,0:T(8,128)S(1)}) custom-call(f32[1024,256]{1,0:T(8,128)} %bitcast.6, f32[8,256]{1,0:T(8,128)} %spread_hbm.1, f32[16,256]{1,0:T(8,128)} %bitcast.7, s32[1,128]{1,0:T(1,128)} %bitcast.8, f32[1,128]{1,0:T(1,128)} %bitcast.9, f32[1,128]{1,0:T(1,128)} %bitcast.10), custom_call_target="tpu_custom_call" | custom-call | tf_op jit(solution)/shard_map/front/pallas_call | solution.py:649
  42.1 5.0 %tail.1 = f32[1024,256]{1,0:T(8,128)} custom-call(f32[72,128]{1,0:T(8,128)S(1)} %get-tuple-element.8.g_ref, f32[8,128,256]{2,1,0:T(8,128)S(1)} %get-tuple-element.9.dd_ref, f32[8,256]{1,0:T(8,128)S(1)} %get-tuple-element.10.mean_ref), custom_call_target="tpu_custom_call" | custom-call | tf_op jit(solution)/shard_map/tail/pallas_call | solution.py:153
